TPU v7x, 32 devices: a whole 2x2x4 slice. The times are simulated.
32 devices in a mesh: groups: 2 (over y), blk: 8 (over z, core), heads: 2 (over x).
Axes of the slice: x: 2, y: 2, z: 4, core: 2. Of those that a mesh axis runs over, the one named last changes fastest.
Arguments:
- span_q: bfloat16 [1024, 5120], P(('groups', 'blk'), 'heads'), parts along dimension 0, may hold values from -12 to 12
- span_k: bfloat16 [1024, 1024], P(('groups', 'blk'), 'heads'), parts along dimension 0, may hold values from -12 to 12
- span_values: bfloat16 [1024, 1024], P(('groups', 'blk'), 'heads'), parts along dimension 0, may hold values from -6 to 6
- cached_keys: bfloat16 [1024, 1024], P(('groups', 'blk'), 'heads'), parts along dimension 0, may hold values from -6 to 6
- cached_values: bfloat16 [1024, 1024], P(('groups', 'blk'), 'heads'), parts along dimension 0, may hold values from -6 to 6
- out_weight: bfloat16 [5120, 5120], P('blk', 'heads'), may hold values from -0.5 to 0.5
- ctx_len: int32 [2], P('groups'), parts along dimension 0, may hold values from 128 to 512
- span_start: int32 [2], P('groups'), parts along dimension 0, may hold values from 512 to 1023
Outputs:
- mixed: bfloat16 [5120, 1024], P('blk', ('groups', 'heads')), parts along dimension 1
There are 2 independent parts, one for each index of `groups`. A program takes and returns all parts, laid end to end along the dimension named above; an argument that names none is the same for every part. Nothing has to cross between parts.
All inputs are finite; a program needn't handle non-finite values.
Results may differ from a plain program's by a relative error of at most 0.014.
Values may be sent and summed in bfloat16 or wider, within the bound.
No kernel may reach another device: no remote copies, remote signals or barrier semaphores. Data moves between devices by JAX's collectives and lax.ppermute only.
A program may use at most 64 MiB of HBM per device.

v0:
```python
import functools
import math

import jax
import jax.numpy as jnp
import numpy as np
from jax import lax
from jax.experimental import pallas as pl
from jax.experimental.pallas import tpu as pltpu
from jax.sharding import PartitionSpec as P


HEAD_SIZE = 128
CORES = 2


ROPE_BASE = 1000000.0
NEG_FILL = -1e30


def whole(space=pltpu.VMEM):
    return pl.BlockSpec(memory_space=space)


def room(mib):
    return pltpu.CompilerParams(vmem_limit_bytes=mib * 1024 * 1024)


def pack_kernel(chips, groups, *refs):
    total = sum(groups)
    arrays, refs = refs[:total], refs[total:]
    chip = lax.axis_index("blk") // CORES
    order = list(reversed(range(chips)))
    taken, given = {}, []
    for g, size in enumerate(groups):
        outs, held, in_sem = refs[g * chips : (g + 1) * chips], refs[g - 3 * len(groups)], refs[g - 2 * len(groups)]
        for j in order:
            taken[g, j] = []
            to = 0
            for n, ref in enumerate(arrays[sum(groups[:g]) : sum(groups[:g]) + size]):
                count = ref.shape[1] // chips
                at = pl.multiple_of((chip ^ j) * count, HEAD_SIZE)
                taken[g, j].append(
                    pltpu.make_async_copy(
                        ref.at[:, pl.ds(at, count)], held.at[j, :, pl.ds(to, count)], in_sem.at[j, n]
                    )
                )
                taken[g, j][-1].start()
                to += count
    for g in range(len(groups)):
        outs, held, out_sem = refs[g * chips : (g + 1) * chips], refs[g - 3 * len(groups)], refs[g - len(groups)]
        for j in order:
            for copy in taken[g, j]:
                copy.wait()
            given.append(pltpu.make_async_copy(held.at[j], outs[j], out_sem.at[j]))
            given[-1].start()
    for copy in given:
        copy.wait()


def pack(chips, *groups):
    slabs = [(group[0].shape[0], sum(x.shape[1] for x in group) // chips) for group in groups]
    out = pl.pallas_call(
        functools.partial(pack_kernel, chips, [len(group) for group in groups]),
        out_shape=[jax.ShapeDtypeStruct(slab, jnp.bfloat16) for slab in slabs for _ in range(chips)],
        in_specs=[whole(pl.ANY) for group in groups for _ in group],
        out_specs=[whole(pl.ANY) for _ in slabs for _ in range(chips)],
        scratch_shapes=[pltpu.VMEM((chips, *slab), jnp.bfloat16) for slab in slabs]
        + [pltpu.SemaphoreType.DMA((chips, len(group))) for group in groups]
        + [pltpu.SemaphoreType.DMA((chips,)) for _ in groups],
        name="pack",
    )(*(x for group in groups for x in group))
    return [out[g * chips : (g + 1) * chips] for g in range(len(groups))]


def attend_kernel(group, own_half, *refs):
    slabs = (len(refs) - 9) // 3
    queries, own, other = refs[:slabs], refs[slabs : 2 * slabs], refs[2 * slabs : 3 * slabs]
    cos_ref, sin_ref, ctx_ref, out_ref, q_s, k_s, v_s, ck_s, cv_s = refs[3 * slabs :]
    me = lax.axis_index("blk")
    chip, core = me // CORES, me % CORES
    rows = own[0].shape[0]
    span = rows * CORES

    def lanes(piece, n):
        return piece[:, n * HEAD_SIZE : (n + 1) * HEAD_SIZE]

    def rotate(x, start):
        x = x.astype(jnp.float32)
        turned = pltpu.roll(x, HEAD_SIZE // 2, 1)
        return (x * cos_ref[pl.ds(start, rows)] + turned * sin_ref[pl.ds(start, rows)]).astype(jnp.bfloat16)

    for j in range(slabs):
        source = chip ^ j
        for piece, side in ((own[j], core), (other[j], 1 - core)):
            at = pl.multiple_of(source * span + side * rows, rows)
            k_s[pl.ds(at, rows)] = rotate(lanes(piece, 0), at)
            v_s[pl.ds(at, rows)] = lanes(piece, 1)
            ck_s[pl.ds(at, rows)] = lanes(piece, 2)
            cv_s[pl.ds(at, rows)] = lanes(piece, 3)
        start = pl.multiple_of(source * span + core * rows, rows)
        for h in range(group):
            at = pl.multiple_of((source * group + h) * rows, rows)
            q_s[pl.ds(at, rows)] = rotate(lanes(queries[j], h), start)

    scale = 1.0 / math.sqrt(HEAD_SIZE)
    height = group * rows
    total_rows = slabs * span
    cached_ok = lax.broadcasted_iota(jnp.int32, (1, total_rows), 1) < ctx_ref[0]
    cached_bias = jnp.where(cached_ok, 0.0, NEG_FILL).astype(jnp.float32)
    row = lax.broadcasted_iota(jnp.int32, (height, span), 0) % rows + core * rows
    col = lax.broadcasted_iota(jnp.int32, (height, span), 1)
    diagonal = col <= row
    contract_last = (((1,), (1,)), ((), ()))

    def attend(blocks):
        for n, block in enumerate(blocks):
            q = q_s[block * height : (block + 1) * height]
            cached = lax.dot_general(q, ck_s[...], contract_last, preferred_element_type=jnp.float32)
            cached = cached * scale + cached_bias
            top = jnp.max(cached, axis=1, keepdims=True)
            parts = [(cached, cv_s[...])]
            if block:
                past = lax.dot_general(
                    q, k_s[: block * span], contract_last, preferred_element_type=jnp.float32
                ) * scale
                top = jnp.maximum(top, jnp.max(past, axis=1, keepdims=True))
                parts.append((past, v_s[: block * span]))
            near = lax.dot_general(
                q, k_s[block * span : (block + 1) * span], contract_last, preferred_element_type=jnp.float32
            ) * scale
            near = jnp.where(diagonal, near, NEG_FILL)
            top = jnp.maximum(top, jnp.max(near, axis=1, keepdims=True))
            parts.append((near, v_s[block * span : (block + 1) * span]))
            total = None
            summed = None
            for scores, values in parts:
                exp_scores = jnp.exp(scores - top)
                part_total = jnp.sum(exp_scores, axis=1, keepdims=True)
                part = jnp.dot(exp_scores.astype(jnp.bfloat16), values, preferred_element_type=jnp.float32)
                total = part_total if total is None else total + part_total
                summed = part if summed is None else summed + part
            result = (summed / total).astype(jnp.bfloat16)
            for h in range(group):
                out_ref[n, :, h * HEAD_SIZE : (h + 1) * HEAD_SIZE] = result[h * rows : (h + 1) * rows]

    half = lax.axis_index("heads")
    for value in range(2):
        which = value if own_half else 1 - value
        blocks = tuple(range(which * slabs // 2, (which + 1) * slabs // 2))
        pl.when(half == value)(functools.partial(attend, blocks))


def project_kernel(picks, w_ref, *refs):
    pieces = len(picks)
    own, other, added = refs[:pieces], refs[pieces : 2 * pieces], refs[2 * pieces : -2]
    out_ref, rows_s = refs[-2:]
    me = lax.axis_index("blk")
    chip, core = me // CORES, me % CORES
    rows, width = own[0].shape[1:]
    for j, blocks in enumerate(picks):
        at = pl.multiple_of((chip ^ j) * width, HEAD_SIZE)
        for piece, side in ((own[j], core), (other[j], 1 - core)):
            for n, block in enumerate(blocks):
                to = pl.multiple_of((n * CORES + side) * rows, rows)
                rows_s[pl.ds(to, rows), pl.ds(at, width)] = piece[block]
    product = lax.dot_general(
        w_ref[...], rows_s[...], (((1,), (1,)), ((), ())), preferred_element_type=jnp.float32
    )
    if not added:
        out_ref[...] = product.astype(jnp.bfloat16)
    for n, ref in enumerate(added):
        count = ref.shape[1]
        lanes = slice(n * count, (n + 1) * count)
        out_ref[:, lanes] = (product[:, lanes] + ref[...].astype(jnp.float32)).astype(jnp.bfloat16)


def head_sharded(chips, span_q, span_k, span_values, cached_keys, cached_values, out_weight, ctx_len, span_start):
    rows = span_q.shape[0]
    group = span_q.shape[1] // span_k.shape[1]
    features = out_weight.shape[0]
    devices = chips * CORES
    total_rows = devices * rows
    width = group * HEAD_SIZE

    def along(j):
        return [(b, b ^ (CORES * j)) for b in range(devices)]

    partner = [(b, b ^ 1) for b in range(devices)]
    across = [(0, 1), (1, 0)]

    keyed, asked = pack(chips, (span_k, span_values, cached_keys, cached_values), (span_q,))
    half_dim = HEAD_SIZE // 2
    inverse = jnp.asarray(np.float32(ROPE_BASE) ** (-(np.arange(half_dim, dtype=np.float32) * 2.0 / HEAD_SIZE)))
    positions = span_start[0] + jnp.arange(total_rows, dtype=jnp.int32)
    angles = positions.astype(jnp.float32)[:, None] * inverse[None, :]
    cosine, sine = jnp.cos(angles), jnp.sin(angles)
    cosine = jnp.concatenate([cosine, cosine], axis=1)
    sine = jnp.concatenate([-sine, sine], axis=1)

    keys = [keyed[0]] + [lax.ppermute(keyed[j], "blk", along(j)) for j in range(1, chips)]
    queries = [asked[0]] + [lax.ppermute(asked[j], "blk", along(j)) for j in range(1, chips)]
    keys[1], cosine, sine = lax.optimization_barrier((keys[1], cosine, sine))
    swapped = [lax.ppermute(x, "blk", partner) for x in keys]
    here = ctx_len[0] >= 0
    keys[0], queries[0] = (jnp.where(here, x, jnp.zeros_like(x)) for x in (keys[0], queries[0]))
    half_chips = chips // 2

    def attend(own_half):
        return pl.pallas_call(
            functools.partial(attend_kernel, group, own_half),
            out_shape=jax.ShapeDtypeStruct((half_chips, rows, width), jnp.bfloat16),
            in_specs=[whole()] * (3 * chips + 2) + [whole(pltpu.SMEM)],
            out_specs=whole(),
            scratch_shapes=[pltpu.VMEM((chips * group * rows, HEAD_SIZE), jnp.bfloat16)]
            + [pltpu.VMEM((total_rows, HEAD_SIZE), jnp.bfloat16)] * 4,
            name="attend",
            compiler_params=room(12),
            cost_estimate=pl.CostEstimate(flops=400_000_000, bytes_accessed=1_000_000, transcendentals=600_000),
        )(*queries, *keys, *swapped, cosine, sine, ctx_len)

    def project(picks, pieces, others, *added):
        count = len(picks[0]) * CORES * rows
        return pl.pallas_call(
            functools.partial(project_kernel, picks),
            out_shape=jax.ShapeDtypeStruct((features, count), jnp.bfloat16),
            in_specs=[whole()] * (1 + 2 * len(pieces) + len(added)),
            out_specs=whole(),
            scratch_shapes=[pltpu.VMEM((count, chips * width), jnp.bfloat16)],
            name="project",
            compiler_params=room(12),
            cost_estimate=pl.CostEstimate(flops=3_000_000 * count, bytes_accessed=8_000 * count, transcendentals=0),
        )(out_weight, *pieces, *others, *added)

    sent = attend(False)
    far = lax.ppermute(sent, "blk", along(2))
    near = lax.ppermute(sent, "blk", along(1))
    pieces = [sent, near, far]
    others = [lax.ppermute(piece, "blk", partner) for piece in pieces]
    received = []
    for n in range(half_chips):
        relayed = lax.ppermute(far[n : n + 1], "blk", along(1))
        other = lax.ppermute(relayed, "blk", partner)
        picks = ((n,), (n,), (n,), (0,))
        partial = project(picks, [*pieces, relayed], [*others, other])
        received.append(lax.ppermute(partial, "heads", across))
    kept = attend(True)
    pieces = [kept] + [lax.ppermute(kept, "blk", along(j)) for j in (1, 2, 3)]
    others = [lax.ppermute(piece, "blk", partner) for piece in pieces]
    return project((tuple(range(half_chips)),) * chips, pieces, others, *received)


def rotary(inputs, positions):
    row_count = inputs.shape[0]
    head_count = inputs.shape[1] // HEAD_SIZE
    floats = inputs.astype(jnp.float32).reshape(row_count, head_count, HEAD_SIZE)
    half_dim = HEAD_SIZE // 2
    inverse = ROPE_BASE ** (-(jnp.arange(half_dim, dtype=jnp.float32) * 2.0 / HEAD_SIZE))
    angles = positions.astype(jnp.float32)[:, None] * inverse[None, :]
    cosine = jnp.cos(angles)[:, None, :]
    sine_val = jnp.sin(angles)[:, None, :]
    first_half = floats[..., :half_dim]
    second_half = floats[..., half_dim:]
    rotated = jnp.concatenate(
        [
            first_half * cosine - second_half * sine_val,
            second_half * cosine + first_half * sine_val,
        ],
        axis=-1,
    )
    return rotated.reshape(row_count, head_count * HEAD_SIZE).astype(jnp.bfloat16)


def token_sharded(span_q, span_k, span_values, cached_keys, cached_values, out_weight, ctx_len, span_start):
    own_index = lax.axis_index("blk")
    local_rows = span_q.shape[0]
    stored_rows = cached_keys.shape[0]
    key_heads = span_k.shape[1] // HEAD_SIZE
    queries_per_group = span_q.shape[1] // span_k.shape[1]
    query_index = own_index * local_rows + jnp.arange(local_rows, dtype=jnp.int32)
    positions = span_start[0] + query_index
    query_rows = rotary(span_q, positions).reshape(
        local_rows, key_heads, queries_per_group, HEAD_SIZE
    )
    new_keys = rotary(span_k, positions)
    cache_limit = ctx_len[0]
    initial = (
        jnp.full((key_heads, queries_per_group, local_rows), NEG_FILL, jnp.float32),
        jnp.zeros((key_heads, queries_per_group, local_rows), jnp.float32),
        jnp.zeros((key_heads, queries_per_group, local_rows, HEAD_SIZE), jnp.float32),
    )
    packed = jnp.concatenate(
        [
            jnp.concatenate([cached_keys, cached_values], axis=1),
            jnp.concatenate([new_keys, span_values], axis=1),
        ],
        axis=0,
    )
    shard_len = stored_rows + local_rows
    key_width = key_heads * HEAD_SIZE
    block_limit = 2560
    running = initial
    piece = lax.all_gather(packed, "blk", axis=0, tiled=True)
    start = jnp.int32(0)
    total_rows = piece.shape[0]
    for row_offset in range(0, total_rows, block_limit):
        row_block = piece[row_offset : row_offset + block_limit]
        row_index = start + row_offset + jnp.arange(row_block.shape[0], dtype=jnp.int32)
        shard_id = row_index // shard_len
        within = row_index % shard_len
        is_cache = within < stored_rows
        cache_pos = shard_id * stored_rows + within
        span_pos = shard_id * local_rows + within - stored_rows
        visible = jnp.where(
            is_cache[None, :],
            (cache_pos < cache_limit)[None, :],
            span_pos[None, :] <= query_index[:, None],
        )
        key_block = row_block[:, :key_width].reshape(-1, key_heads, HEAD_SIZE)
        value_block = row_block[:, key_width:].reshape(-1, key_heads, HEAD_SIZE)
        scores = jnp.einsum(
            "qgkd,tgd->gkqt", query_rows, key_block, preferred_element_type=jnp.float32
        ) / math.sqrt(HEAD_SIZE)
        scores = jnp.where(visible[None, None], scores, NEG_FILL)
        attend_largest, attend_denominator, attend_weighted = running
        new_largest = jnp.maximum(attend_largest, jnp.max(scores, axis=-1))
        shrink = jnp.exp(attend_largest - new_largest)
        exp_scores = jnp.exp(scores - new_largest[..., None])
        attend_denominator = attend_denominator * shrink + jnp.sum(exp_scores, axis=-1)
        product = jnp.einsum(
            "gkqt,tgd->gkqd",
            exp_scores.astype(jnp.bfloat16),
            value_block,
            preferred_element_type=jnp.float32,
        )
        attend_weighted = attend_weighted * shrink[..., None] + product
        running = (new_largest, attend_denominator, attend_weighted)
    _, denominator, weighted = running
    normalized = weighted / denominator[..., None]
    attended = (
        jnp.transpose(normalized, (2, 0, 1, 3))
        .reshape(local_rows, key_heads * queries_per_group * HEAD_SIZE)
        .astype(jnp.bfloat16)
    )
    partial_value = lax.dot_general(
        out_weight,
        lax.all_gather(attended, "blk", axis=0, tiled=True),
        (((1,), (1,)), ((), ())),
        preferred_element_type=jnp.float32,
    )
    summed = lax.psum_scatter(
        partial_value.astype(jnp.bfloat16), "heads", scatter_dimension=1, tiled=True
    )
    return summed


def local(blk, heads, span_q, span_k, *others):
    chips = blk // CORES
    key_heads = span_k.shape[1] // HEAD_SIZE
    if by_head(blk, heads, key_heads):
        return head_sharded(chips, span_q, span_k, *others)
    return token_sharded(span_q, span_k, *others)


def by_head(blk, heads, key_heads):
    return blk == CORES * key_heads and key_heads == 4 and heads == 2


def solution(mesh):
    placed = (
        P(("groups", "blk"), "heads"),
        P(("groups", "blk"), "heads"),
        P(("groups", "blk"), "heads"),
        P(("groups", "blk"), "heads"),
        P(("groups", "blk"), "heads"),
        P("blk", "heads"),
        P("groups"),
        P("groups"),
    )
    return jax.shard_map(
        functools.partial(local, mesh.shape["blk"], mesh.shape["heads"]),
        mesh=mesh,
        in_specs=placed,
        out_specs=P("blk", ("groups", "heads")),
        check_vma=False,
    )
```

profile of v0, /device:TPU:0, one launch (start us, length us, event | category | flops | bytes accessed | tf_op | source)
XLA Modules:
  0.0 70.6 jit_solution(10929646650423509743)
XLA Ops:
  0.0 2.2 %pack.1 = (bf16[64,512]{1,0:T(8,128)(2,1)}, bf16[64,512]{1,0:T(8,128)(2,1)}, bf16[64,512]{1,0:T(8,128)(2,1)}, bf16[64,512]{1,0:T(8,128)(2,1)}, bf16[64,640]{1,0:...) custom-call(bf16[64,512]{1,0:T(8,128)(2,1)} %refs_0_.1, ...), custom_call_target="tpu_custom_call" | custom-call | tf_op jit(solution)/shard_map/pack/pallas_call | solution.py:63
  2.2 3.1 %collective-permute-start.3 = (bf16[64,512]{1,0:T(8,128)(2,1)}, bf16[64,512]{1,0:T(8,128)(2,1)S(1)}, u32[]{:S(2)}, u32[]{:S(2)}) collective-permute-start(bf16[64,512]{1,0:T(8,128)(2,1)} %get-tuple-element.21), channel_id=1, source_target_pairs={{0,4},{2,6},{4,0},{6,2},{8,12},{10,14},{12,8},{14,10},{1,5},{3,7},... | collective-permute-start | bytes 196616 | tf_op jit(solution)/shard_map/ppermute | solution.py:201
  5.3 2.6 %collective-permute-start.4 = (bf16[64,512]{1,0:T(8,128)(2,1)}, bf16[64,512]{1,0:T(8,128)(2,1)S(1)}, u32[]{:S(2)}, u32[]{:S(2)}) collective-permute-start(bf16[64,512]{1,0:T(8,128)(2,1)} %get-tuple-element.23), channel_id=1, source_target_pairs={{0,8},{2,10},{4,12},{6,14},{8,0},{10,2},{12,4},{14,6},{1,9},{3,11}... | collective-permute-start | bytes 196616 | tf_op jit(solution)/shard_map/ppermute | solution.py:201
  7.9 0.9 %collective-permute-start = (bf16[64,640]{1,0:T(8,128)(2,1)}, bf16[64,640]{1,0:T(8,128)(2,1)S(1)}, u32[]{:S(2)}, u32[]{:S(2)}) collective-permute-start(bf16[64,640]{1,0:T(8,128)(2,1)} %get-tuple-element.17), channel_id=1, source_target_pairs={{0,4},{2,6},{4,0},{6,2},{8,12},{10,14},{12,8},{14,10},{1,5},{3,7},... | collective-permute-start | bytes 245768 | tf_op jit(solution)/shard_map/ppermute | solution.py:202
  10.1 0.9 %broadcast_select_fusion.refs_0_ = bf16[64,640]{1,0:T(8,128)(2,1)S(1)} fusion(bf16[64,640]{1,0:T(8,128)(2,1)} %get-tuple-element.16, pred[]{:T(512)} %bitcast), kind=kLoop, calls=%fused_computation.5 | loop fusion | flops 40960 | bytes 163841 | tf_op jit(solution)/shard_map/jit(_where)/select_n | solution.py:206
  11.0 1.6 %fusion = (f32[512,64]{1,0:T(8,128)S(1)}, f32[512,64]{1,0:T(8,128)S(1)}, f32[512,64]{1,0:T(8,128)S(1)}) fusion(f32[64]{0:T(128)} %constant.8.clone, f32[512]{0:T(512)S(1)} %add_convert_fusion), kind=kLoop, calls=%fused_computation.4 | loop fusion | flops 65536 | bytes 395520 | tf_op jit(solution)/shard_map/neg | solution.py:199
  12.7 0.2 pad_maximum_fusion
  12.9 3.6 %collective-permute-start.1 = (bf16[64,640]{1,0:T(8,128)(2,1)}, bf16[64,640]{1,0:T(8,128)(2,1)S(1)}, u32[]{:S(2)}, u32[]{:S(2)}) collective-permute-start(bf16[64,640]{1,0:T(8,128)(2,1)} %get-tuple-element.18), channel_id=1, source_target_pairs={{0,8},{2,10},{4,12},{6,14},{8,0},{10,2},{12,4},{14,6},{1,9},{3,11}... | collective-permute-start | bytes 245768 | tf_op jit(solution)/shard_map/ppermute | solution.py:202
  16.5 0.0 collective-permute-done.4.refs_6_
  16.5 0.0 collective-permute-start.2
  16.5 0.0 collective-permute-done.5.refs_7_
  16.5 0.1 collective-permute-start.7
  16.6 0.5 collective-permute-start.8
  17.1 0.0 collective-permute-done.refs_1_
  17.1 0.1 collective-permute-start.9
  17.2 0.8 %broadcast_select_fusion.1.refs_4_ = bf16[64,512]{1,0:T(8,128)(2,1)S(1)} fusion(bf16[64,512]{1,0:T(8,128)(2,1)} %get-tuple-element.20, pred[]{:T(512)} %bitcast), kind=kLoop, calls=%fused_computation.6 | loop fusion | flops 32768 | bytes 131073 | tf_op jit(solution)/shard_map/jit(_where)/select_n | solution.py:206
  18.0 3.0 %collective-permute-done.1.refs_2_ = bf16[64,640]{1,0:T(8,128)(2,1)S(1)} collective-permute-done((bf16[64,640]{1,0:T(8,128)(2,1)}, bf16[64,640]{1,0:T(8,128)(2,1)S(1)}, u32[]{:S(2)}, u32[]{:S(2)}) %collective-permute-start.1) | collective-permute-done | bytes 81952 | tf_op jit(solution)/shard_map/ppermute | solution.py:202
  21.0 1.9 %collective-permute-done.2.refs_3_ = bf16[64,640]{1,0:T(8,128)(2,1)S(1)} collective-permute-done((bf16[64,640]{1,0:T(8,128)(2,1)}, bf16[64,640]{1,0:T(8,128)(2,1)S(1)}, u32[]{:S(2)}, u32[]{:S(2)}) %collective-permute-start.2) | collective-permute-done | bytes 81952 | tf_op jit(solution)/shard_map/ppermute | solution.py:202
  22.9 1.6 %attend.3.refs_0_ = bf16[2,64,640]{2,1,0:T(8,128)(2,1)S(1)} custom-call(bf16[64,640]{1,0:T(8,128)(2,1)S(1)} %broadcast_select_fusion.refs_0_, bf16[64,640]{1,0:T(8,128)(2,1)S(1)} %collective-permute-done.refs_1_, bf16[64,640]{1,0:T(8,128)(2,1)S(1)} %collective-permute-done.1.refs_2_, bf16[64,640]{1,0:T(8,128)(2,1)S(1)} %collective-permute-done.2.refs_3_, ...), custom_call_target="tpu_custom_call" | custom-call | flops 400000000 | bytes 1000000 | tf_op jit(solution)/shard_map/attend/pallas_call | solution.py:210
  24.6 3.4 %collective-permute-start.18 = (bf16[2,64,640]{2,1,0:T(8,128)(2,1)S(1)}, bf16[2,64,640]{2,1,0:T(8,128)(2,1)S(1)}, u32[]{:S(2)}, u32[]{:S(2)}) collective-permute-start(bf16[2,64,640]{2,1,0:T(8,128)(2,1)S(1)} %attend.3.refs_0_), channel_id=1, source_target_pairs={{0,8},{2,10},{4,12},{6,14},{8,0},{10,2},{12,4},{14,6},{1,9},{3,11}... | collective-permute-start | bytes 491528 | tf_op jit(solution)/shard_map/ppermute | solution.py:236
  28.0 1.4 %attend.2.refs_0_ = bf16[2,64,640]{2,1,0:T(8,128)(2,1)S(1)} custom-call(bf16[64,640]{1,0:T(8,128)(2,1)S(1)} %broadcast_select_fusion.refs_0_, bf16[64,640]{1,0:T(8,128)(2,1)S(1)} %collective-permute-done.refs_1_, bf16[64,640]{1,0:T(8,128)(2,1)S(1)} %collective-permute-done.1.refs_2_, bf16[64,640]{1,0:T(8,128)(2,1)S(1)} %collective-permute-done.2.refs_3_, ...), custom_call_target="tpu_custom_call" | custom-call | flops 400000000 | bytes 1000000 | tf_op jit(solution)/shard_map/attend/pallas_call | solution.py:210
  29.4 1.3 %collective-permute-start.12 = (bf16[2,64,640]{2,1,0:T(8,128)(2,1)S(1)}, bf16[2,64,640]{2,1,0:T(8,128)(2,1)S(1)}, u32[]{:S(2)}, u32[]{:S(2)}) collective-permute-start(bf16[2,64,640]{2,1,0:T(8,128)(2,1)S(1)} %attend.2.refs_0_), channel_id=1, source_target_pairs={{0,12},{2,14},{4,8},{6,10},{8,4},{10,6},{12,0},{14,2},{1,13},{3,15... | collective-permute-start | bytes 491528 | tf_op jit(solution)/shard_map/ppermute | solution.py:248
  30.7 0.5 collective-permute-start.11
  31.1 2.7 %collective-permute-start.10 = (bf16[2,64,640]{2,1,0:T(8,128)(2,1)S(1)}, bf16[2,64,640]{2,1,0:T(8,128)(2,1)S(1)}, u32[]{:S(2)}, u32[]{:S(2)}) collective-permute-start(bf16[2,64,640]{2,1,0:T(8,128)(2,1)S(1)} %attend.2.refs_0_), channel_id=1, source_target_pairs={{0,4},{2,6},{4,0},{6,2},{8,12},{10,14},{12,8},{14,10},{1,5},{3,7},... | collective-permute-start | bytes 491528 | tf_op jit(solution)/shard_map/ppermute | solution.py:248
  33.9 9.7 %collective-permute-done.18.refs_2_ = bf16[2,64,640]{2,1,0:T(8,128)(2,1)S(1)} collective-permute-done((bf16[2,64,640]{2,1,0:T(8,128)(2,1)S(1)}, bf16[2,64,640]{2,1,0:T(8,128)(2,1)S(1)}, u32[]{:S(2)}, u32[]{:S(2)}) %collective-permute-start.18) | collective-permute-done | bytes 163872 | tf_op jit(solution)/shard_map/ppermute | solution.py:236
  43.6 0.0 collective-permute-start.17
  43.6 0.0 collective-permute-done.12.refs_3_
  43.6 4.0 %collective-permute-start.19 = (bf16[1,64,640]{2,1,0:T(8,128)(2,1)S(1)}, bf16[1,64,640]{2,1,0:T(8,128)(2,1)S(1)}, u32[]{:S(2)}, u32[]{:S(2)}) collective-permute-start(bf16[1,64,640]{2,1,0:T(8,128)(2,1)S(1)} %get-tuple-element.28), channel_id=1, source_target_pairs={{0,4},{2,6},{4,0},{6,2},{8,12},{10,14},{12,8},{14,10},{1,5},{3,7},... | collective-permute-start | bytes 245768 | tf_op jit(solution)/shard_map/ppermute | solution.py:242
  47.7 2.0 %collective-permute-done.11.refs_2_ = bf16[2,64,640]{2,1,0:T(8,128)(2,1)S(1)} collective-permute-done((bf16[2,64,640]{2,1,0:T(8,128)(2,1)S(1)}, bf16[2,64,640]{2,1,0:T(8,128)(2,1)S(1)}, u32[]{:S(2)}, u32[]{:S(2)}) %collective-permute-start.11) | collective-permute-done | bytes 163872 | tf_op jit(solution)/shard_map/ppermute | solution.py:248
  49.7 2.3 %collective-permute-done.17.refs_1_ = bf16[2,64,640]{2,1,0:T(8,128)(2,1)S(1)} collective-permute-done((bf16[2,64,640]{2,1,0:T(8,128)(2,1)S(1)}, bf16[2,64,640]{2,1,0:T(8,128)(2,1)S(1)}, u32[]{:S(2)}, u32[]{:S(2)}) %collective-permute-start.17) | collective-permute-done | bytes 163872 | tf_op jit(solution)/shard_map/ppermute | solution.py:237
  51.9 0.0 collective-permute-start.21
  51.9 0.0 collective-permute-done.10.refs_1_
  51.9 0.0 collective-permute-start.25
  52.0 0.6 collective-permute-start.13
  52.5 0.3 collective-permute-done.19.refs_3_
  52.8 0.0 collective-permute-start.23
  52.8 4.0 %collective-permute-done.25.refs_3_ = bf16[1,64,640]{2,1,0:T(8,128)(2,1)S(1)} collective-permute-done((bf16[1,64,640]{2,1,0:T(8,128)(2,1)S(1)}, bf16[1,64,640]{2,1,0:T(8,128)(2,1)S(1)}, u32[]{:S(2)}, u32[]{:S(2)}) %collective-permute-start.25) | collective-permute-done | bytes 81952 | tf_op jit(solution)/shard_map/ppermute | solution.py:242
  56.8 0.5 collective-permute-start.16
  57.3 0.0 collective-permute-done.22.refs_6_
  57.3 0.1 collective-permute-start.15
  57.4 0.4 collective-permute-start.14
  57.8 1.1 %project.3 = bf16[640,128]{1,0:T(8,128)(2,1)S(1)} custom-call(bf16[640,2560]{1,0:T(8,128)(2,1)S(1)} %copy-done, bf16[2,64,640]{2,1,0:T(8,128)(2,1)S(1)} %attend.3.refs_0_, bf16[2,64,640]{2,1,0:T(8,128)(2,1)S(1)} %collective-permute-done.17.refs_1_, bf16[2,64,640]{2,1,0:T(8,128)(2,1)S(1)} %collective-permute-done.18.refs_2_, ...), custom_call_target="tpu_custom_call" | custom-call | flops 384000000 | bytes 1024000 | tf_op jit(solution)/shard_map/project/pallas_call | solution.py:224
  58.9 1.4 %collective-permute-start.24 = (bf16[640,128]{1,0:T(8,128)(2,1)S(1)}, bf16[640,128]{1,0:T(8,128)(2,1)S(1)}, u32[]{:S(2)}, u32[]{:S(2)}) collective-permute-start(bf16[640,128]{1,0:T(8,128)(2,1)S(1)} %project.3), channel_id=1, source_target_pairs={{0,1},{1,0},{2,3},{3,2},{4,5},{5,4},{6,7},{7,6},{8,9},{9,8},{10,11... | collective-permute-start | bytes 491528 | tf_op jit(solution)/shard_map/ppermute | solution.py:246
  60.3 1.1 %project.4 = bf16[640,128]{1,0:T(8,128)(2,1)S(1)} custom-call(bf16[640,2560]{1,0:T(8,128)(2,1)S(1)} %copy-done, bf16[2,64,640]{2,1,0:T(8,128)(2,1)S(1)} %attend.3.refs_0_, bf16[2,64,640]{2,1,0:T(8,128)(2,1)S(1)} %collective-permute-done.17.refs_1_, bf16[2,64,640]{2,1,0:T(8,128)(2,1)S(1)} %collective-permute-done.18.refs_2_, ...), custom_call_target="tpu_custom_call" | custom-call | flops 384000000 | bytes 1024000 | tf_op jit(solution)/shard_map/project/pallas_call | solution.py:224
  61.4 0.8 %collective-permute-start.27 = (bf16[640,128]{1,0:T(8,128)(2,1)S(1)}, bf16[640,128]{1,0:T(8,128)(2,1)S(1)}, u32[]{:S(2)}, u32[]{:S(2)}) collective-permute-start(bf16[640,128]{1,0:T(8,128)(2,1)S(1)} %project.4), channel_id=1, source_target_pairs={{0,1},{1,0},{2,3},{3,2},{4,5},{5,4},{6,7},{7,6},{8,9},{9,8},{10,11... | collective-permute-start | bytes 491528 | tf_op jit(solution)/shard_map/ppermute | solution.py:246
  62.2 3.9 %collective-permute-done.24.refs_8_ = bf16[640,128]{1,0:T(8,128)(2,1)S(1)} collective-permute-done((bf16[640,128]{1,0:T(8,128)(2,1)S(1)}, bf16[640,128]{1,0:T(8,128)(2,1)S(1)}, u32[]{:S(2)}, u32[]{:S(2)}) %collective-permute-start.24) | collective-permute-done | bytes 163872 | tf_op jit(solution)/shard_map/ppermute | solution.py:246
  66.1 2.6 %collective-permute-done.27.refs_9_ = bf16[640,128]{1,0:T(8,128)(2,1)S(1)} collective-permute-done((bf16[640,128]{1,0:T(8,128)(2,1)S(1)}, bf16[640,128]{1,0:T(8,128)(2,1)S(1)}, u32[]{:S(2)}, u32[]{:S(2)}) %collective-permute-start.27) | collective-permute-done | bytes 163872 | tf_op jit(solution)/shard_map/ppermute | solution.py:246
  68.7 1.9 %project.5 = bf16[640,256]{1,0:T(8,128)(2,1)} custom-call(bf16[640,2560]{1,0:T(8,128)(2,1)S(1)} %copy-done, bf16[2,64,640]{2,1,0:T(8,128)(2,1)S(1)} %attend.2.refs_0_, bf16[2,64,640]{2,1,0:T(8,128)(2,1)S(1)} %collective-permute-done.10.refs_1_, bf16[2,64,640]{2,1,0:T(8,128)(2,1)S(1)} %collective-permute-done.11.refs_2_, ...), custom_call_target="tpu_custom_call" | custom-call | flops 768000000 | bytes 2048000 | tf_op jit(solution)/shard_map/project/pallas_call | solution.py:224
  (22 shorter events, 0.1 us)
Async XLA Ops:
  0.0 57.8 %copy-start = (bf16[640,2560]{1,0:T(8,128)(2,1)S(1)}, bf16[640,2560]{1,0:T(8,128)(2,1)}, u32[]{:S(2)}) copy-start(bf16[640,2560]{1,0:T(8,128)(2,1)} %w_ref.5) | copy-start | bytes 9830404
  2.2 10.7 %collective-permute-start.3 = (bf16[64,512]{1,0:T(8,128)(2,1)}, bf16[64,512]{1,0:T(8,128)(2,1)S(1)}, u32[]{:S(2)}, u32[]{:S(2)}) collective-permute-start(bf16[64,512]{1,0:T(8,128)(2,1)} %get-tuple-element.21), channel_id=1, source_target_pairs={{0,4},{2,6},{4,0},{6,2},{8,12},{10,14},{12,8},{14,10},{1,5},{3,7},... | collective-permute-start | bytes 196616 | tf_op jit(solution)/shard_map/ppermute | solution.py:201
  5.3 11.1 %collective-permute-start.4 = (bf16[64,512]{1,0:T(8,128)(2,1)}, bf16[64,512]{1,0:T(8,128)(2,1)S(1)}, u32[]{:S(2)}, u32[]{:S(2)}) collective-permute-start(bf16[64,512]{1,0:T(8,128)(2,1)} %get-tuple-element.23), channel_id=1, source_target_pairs={{0,8},{2,10},{4,12},{6,14},{8,0},{10,2},{12,4},{14,6},{1,9},{3,11}... | collective-permute-start | bytes 196616 | tf_op jit(solution)/shard_map/ppermute | solution.py:201
  7.9 8.6 %collective-permute-start.5 = (bf16[64,512]{1,0:T(8,128)(2,1)}, bf16[64,512]{1,0:T(8,128)(2,1)S(1)}, u32[]{:S(2)}, u32[]{:S(2)}) collective-permute-start(bf16[64,512]{1,0:T(8,128)(2,1)} %get-tuple-element.24), channel_id=1, source_target_pairs={{0,12},{2,14},{4,8},{6,10},{8,4},{10,6},{12,0},{14,2},{1,13},{3,15... | collective-permute-start | bytes 196616 | tf_op jit(solution)/shard_map/ppermute | solution.py:201
  7.9 8.6 %collective-permute-start.6 = (bf16[64,512]{1,0:T(8,128)(2,1)}, bf16[64,512]{1,0:T(8,128)(2,1)S(1)}, u32[]{:S(2)}, u32[]{:S(2)}) collective-permute-start(bf16[64,512]{1,0:T(8,128)(2,1)} %get-tuple-element.20), channel_id=1, source_target_pairs={{0,2},{2,0},{4,6},{6,4},{8,10},{10,8},{12,14},{14,12},{1,3},{3,1},... | collective-permute-start | bytes 196616 | tf_op jit(solution)/shard_map/ppermute | solution.py:204
  7.9 9.1 %collective-permute-start = (bf16[64,640]{1,0:T(8,128)(2,1)}, bf16[64,640]{1,0:T(8,128)(2,1)S(1)}, u32[]{:S(2)}, u32[]{:S(2)}) collective-permute-start(bf16[64,640]{1,0:T(8,128)(2,1)} %get-tuple-element.17), channel_id=1, source_target_pairs={{0,4},{2,6},{4,0},{6,2},{8,12},{10,14},{12,8},{14,10},{1,5},{3,7},... | collective-permute-start | bytes 245768 | tf_op jit(solution)/shard_map/ppermute | solution.py:202
  12.9 8.1 %collective-permute-start.1 = (bf16[64,640]{1,0:T(8,128)(2,1)}, bf16[64,640]{1,0:T(8,128)(2,1)S(1)}, u32[]{:S(2)}, u32[]{:S(2)}) collective-permute-start(bf16[64,640]{1,0:T(8,128)(2,1)} %get-tuple-element.18), channel_id=1, source_target_pairs={{0,8},{2,10},{4,12},{6,14},{8,0},{10,2},{12,4},{14,6},{1,9},{3,11}... | collective-permute-start | bytes 245768 | tf_op jit(solution)/shard_map/ppermute | solution.py:202
  16.5 6.5 %collective-permute-start.2 = (bf16[64,640]{1,0:T(8,128)(2,1)}, bf16[64,640]{1,0:T(8,128)(2,1)S(1)}, u32[]{:S(2)}, u32[]{:S(2)}) collective-permute-start(bf16[64,640]{1,0:T(8,128)(2,1)} %get-tuple-element.19), channel_id=1, source_target_pairs={{0,12},{2,14},{4,8},{6,10},{8,4},{10,6},{12,0},{14,2},{1,13},{3,15... | collective-permute-start | bytes 245768 | tf_op jit(solution)/shard_map/ppermute | solution.py:202
  16.5 6.5 %collective-permute-start.7 = (bf16[64,512]{1,0:T(8,128)(2,1)S(1)}, bf16[64,512]{1,0:T(8,128)(2,1)S(1)}, u32[]{:S(2)}, u32[]{:S(2)}) collective-permute-start(bf16[64,512]{1,0:T(8,128)(2,1)S(1)} %collective-permute-done.3.refs_5_), channel_id=1, source_target_pairs={{0,2},{2,0},{4,6},{6,4},{8,10},{10,8},{12,14},{14,12},{1,3},{3,1},... | collective-permute-start | bytes 196616 | tf_op jit(solution)/shard_map/ppermute | solution.py:204
  16.6 6.4 %collective-permute-start.8 = (bf16[64,512]{1,0:T(8,128)(2,1)S(1)}, bf16[64,512]{1,0:T(8,128)(2,1)S(1)}, u32[]{:S(2)}, u32[]{:S(2)}) collective-permute-start(bf16[64,512]{1,0:T(8,128)(2,1)S(1)} %collective-permute-done.4.refs_6_), channel_id=1, source_target_pairs={{0,2},{2,0},{4,6},{6,4},{8,10},{10,8},{12,14},{14,12},{1,3},{3,1},... | collective-permute-start | bytes 196616 | tf_op jit(solution)/shard_map/ppermute | solution.py:204
  17.1 5.9 %collective-permute-start.9 = (bf16[64,512]{1,0:T(8,128)(2,1)S(1)}, bf16[64,512]{1,0:T(8,128)(2,1)S(1)}, u32[]{:S(2)}, u32[]{:S(2)}) collective-permute-start(bf16[64,512]{1,0:T(8,128)(2,1)S(1)} %collective-permute-done.5.refs_7_), channel_id=1, source_target_pairs={{0,2},{2,0},{4,6},{6,4},{8,10},{10,8},{12,14},{14,12},{1,3},{3,1},... | collective-permute-start | bytes 196616 | tf_op jit(solution)/shard_map/ppermute | solution.py:204
  24.6 19.0 %collective-permute-start.18 = (bf16[2,64,640]{2,1,0:T(8,128)(2,1)S(1)}, bf16[2,64,640]{2,1,0:T(8,128)(2,1)S(1)}, u32[]{:S(2)}, u32[]{:S(2)}) collective-permute-start(bf16[2,64,640]{2,1,0:T(8,128)(2,1)S(1)} %attend.3.refs_0_), channel_id=1, source_target_pairs={{0,8},{2,10},{4,12},{6,14},{8,0},{10,2},{12,4},{14,6},{1,9},{3,11}... | collective-permute-start | bytes 491528 | tf_op jit(solution)/shard_map/ppermute | solution.py:236
  29.4 14.2 %collective-permute-start.12 = (bf16[2,64,640]{2,1,0:T(8,128)(2,1)S(1)}, bf16[2,64,640]{2,1,0:T(8,128)(2,1)S(1)}, u32[]{:S(2)}, u32[]{:S(2)}) collective-permute-start(bf16[2,64,640]{2,1,0:T(8,128)(2,1)S(1)} %attend.2.refs_0_), channel_id=1, source_target_pairs={{0,12},{2,14},{4,8},{6,10},{8,4},{10,6},{12,0},{14,2},{1,13},{3,15... | collective-permute-start | bytes 491528 | tf_op jit(solution)/shard_map/ppermute | solution.py:248
  30.7 19.0 %collective-permute-start.11 = (bf16[2,64,640]{2,1,0:T(8,128)(2,1)S(1)}, bf16[2,64,640]{2,1,0:T(8,128)(2,1)S(1)}, u32[]{:S(2)}, u32[]{:S(2)}) collective-permute-start(bf16[2,64,640]{2,1,0:T(8,128)(2,1)S(1)} %attend.2.refs_0_), channel_id=1, source_target_pairs={{0,8},{2,10},{4,12},{6,14},{8,0},{10,2},{12,4},{14,6},{1,9},{3,11}... | collective-permute-start | bytes 491528 | tf_op jit(solution)/shard_map/ppermute | solution.py:248
  31.1 20.8 %collective-permute-start.10 = (bf16[2,64,640]{2,1,0:T(8,128)(2,1)S(1)}, bf16[2,64,640]{2,1,0:T(8,128)(2,1)S(1)}, u32[]{:S(2)}, u32[]{:S(2)}) collective-permute-start(bf16[2,64,640]{2,1,0:T(8,128)(2,1)S(1)} %attend.2.refs_0_), channel_id=1, source_target_pairs={{0,4},{2,6},{4,0},{6,2},{8,12},{10,14},{12,8},{14,10},{1,5},{3,7},... | collective-permute-start | bytes 491528 | tf_op jit(solution)/shard_map/ppermute | solution.py:248
  33.9 18.1 %collective-permute-start.20 = (bf16[2,64,640]{2,1,0:T(8,128)(2,1)S(1)}, bf16[2,64,640]{2,1,0:T(8,128)(2,1)S(1)}, u32[]{:S(2)}, u32[]{:S(2)}) collective-permute-start(bf16[2,64,640]{2,1,0:T(8,128)(2,1)S(1)} %attend.3.refs_0_), channel_id=1, source_target_pairs={{0,2},{2,0},{4,6},{6,4},{8,10},{10,8},{12,14},{14,12},{1,3},{3,1},... | collective-permute-start | bytes 491528 | tf_op jit(solution)/shard_map/ppermute | solution.py:239
  43.6 8.3 %collective-permute-start.17 = (bf16[2,64,640]{2,1,0:T(8,128)(2,1)S(1)}, bf16[2,64,640]{2,1,0:T(8,128)(2,1)S(1)}, u32[]{:S(2)}, u32[]{:S(2)}) collective-permute-start(bf16[2,64,640]{2,1,0:T(8,128)(2,1)S(1)} %attend.3.refs_0_), channel_id=1, source_target_pairs={{0,4},{2,6},{4,0},{6,2},{8,12},{10,14},{12,8},{14,10},{1,5},{3,7},... | collective-permute-start | bytes 491528 | tf_op jit(solution)/shard_map/ppermute | solution.py:237
  43.6 9.2 %collective-permute-start.19 = (bf16[1,64,640]{2,1,0:T(8,128)(2,1)S(1)}, bf16[1,64,640]{2,1,0:T(8,128)(2,1)S(1)}, u32[]{:S(2)}, u32[]{:S(2)}) collective-permute-start(bf16[1,64,640]{2,1,0:T(8,128)(2,1)S(1)} %get-tuple-element.28), channel_id=1, source_target_pairs={{0,4},{2,6},{4,0},{6,2},{8,12},{10,14},{12,8},{14,10},{1,5},{3,7},... | collective-permute-start | bytes 245768 | tf_op jit(solution)/shard_map/ppermute | solution.py:242
  49.7 7.6 %collective-permute-start.22 = (bf16[2,64,640]{2,1,0:T(8,128)(2,1)S(1)}, bf16[2,64,640]{2,1,0:T(8,128)(2,1)S(1)}, u32[]{:S(2)}, u32[]{:S(2)}) collective-permute-start(bf16[2,64,640]{2,1,0:T(8,128)(2,1)S(1)} %collective-permute-done.18.refs_2_), channel_id=1, source_target_pairs={{0,2},{2,0},{4,6},{6,4},{8,10},{10,8},{12,14},{14,12},{1,3},{3,1},... | collective-permute-start | bytes 491528 | tf_op jit(solution)/shard_map/ppermute | solution.py:239
  51.9 5.5 %collective-permute-start.21 = (bf16[2,64,640]{2,1,0:T(8,128)(2,1)S(1)}, bf16[2,64,640]{2,1,0:T(8,128)(2,1)S(1)}, u32[]{:S(2)}, u32[]{:S(2)}) collective-permute-start(bf16[2,64,640]{2,1,0:T(8,128)(2,1)S(1)} %collective-permute-done.17.refs_1_), channel_id=1, source_target_pairs={{0,2},{2,0},{4,6},{6,4},{8,10},{10,8},{12,14},{14,12},{1,3},{3,1},... | collective-permute-start | bytes 491528 | tf_op jit(solution)/shard_map/ppermute | solution.py:239
  51.9 4.9 %collective-permute-start.25 = (bf16[1,64,640]{2,1,0:T(8,128)(2,1)S(1)}, bf16[1,64,640]{2,1,0:T(8,128)(2,1)S(1)}, u32[]{:S(2)}, u32[]{:S(2)}) collective-permute-start(bf16[1,64,640]{2,1,0:T(8,128)(2,1)S(1)} %get-tuple-element.27), channel_id=1, source_target_pairs={{0,4},{2,6},{4,0},{6,2},{8,12},{10,14},{12,8},{14,10},{1,5},{3,7},... | collective-permute-start | bytes 245768 | tf_op jit(solution)/shard_map/ppermute | solution.py:242
  52.0 9.4 %collective-permute-start.13 = (bf16[2,64,640]{2,1,0:T(8,128)(2,1)S(1)}, bf16[2,64,640]{2,1,0:T(8,128)(2,1)S(1)}, u32[]{:S(2)}, u32[]{:S(2)}) collective-permute-start(bf16[2,64,640]{2,1,0:T(8,128)(2,1)S(1)} %attend.2.refs_0_), channel_id=1, source_target_pairs={{0,2},{2,0},{4,6},{6,4},{8,10},{10,8},{12,14},{14,12},{1,3},{3,1},... | collective-permute-start | bytes 491528 | tf_op jit(solution)/shard_map/ppermute | solution.py:249
  52.8 4.0 %collective-permute-start.23 = (bf16[1,64,640]{2,1,0:T(8,128)(2,1)S(1)}, bf16[1,64,640]{2,1,0:T(8,128)(2,1)S(1)}, u32[]{:S(2)}, u32[]{:S(2)}) collective-permute-start(bf16[1,64,640]{2,1,0:T(8,128)(2,1)S(1)} %collective-permute-done.19.refs_3_), channel_id=1, source_target_pairs={{0,2},{2,0},{4,6},{6,4},{8,10},{10,8},{12,14},{14,12},{1,3},{3,1},... | collective-permute-start | bytes 245768 | tf_op jit(solution)/shard_map/ppermute | solution.py:243
  56.8 2.1 %collective-permute-start.26 = (bf16[1,64,640]{2,1,0:T(8,128)(2,1)S(1)}, bf16[1,64,640]{2,1,0:T(8,128)(2,1)S(1)}, u32[]{:S(2)}, u32[]{:S(2)}) collective-permute-start(bf16[1,64,640]{2,1,0:T(8,128)(2,1)S(1)} %collective-permute-done.25.refs_3_), channel_id=1, source_target_pairs={{0,2},{2,0},{4,6},{6,4},{8,10},{10,8},{12,14},{14,12},{1,3},{3,1},... | collective-permute-start | bytes 245768 | tf_op jit(solution)/shard_map/ppermute | solution.py:243
  56.8 5.4 %collective-permute-start.16 = (bf16[2,64,640]{2,1,0:T(8,128)(2,1)S(1)}, bf16[2,64,640]{2,1,0:T(8,128)(2,1)S(1)}, u32[]{:S(2)}, u32[]{:S(2)}) collective-permute-start(bf16[2,64,640]{2,1,0:T(8,128)(2,1)S(1)} %collective-permute-done.12.refs_3_), channel_id=1, source_target_pairs={{0,2},{2,0},{4,6},{6,4},{8,10},{10,8},{12,14},{14,12},{1,3},{3,1},... | collective-permute-start | bytes 491528 | tf_op jit(solution)/shard_map/ppermute | solution.py:249
  57.3 4.9 %collective-permute-start.15 = (bf16[2,64,640]{2,1,0:T(8,128)(2,1)S(1)}, bf16[2,64,640]{2,1,0:T(8,128)(2,1)S(1)}, u32[]{:S(2)}, u32[]{:S(2)}) collective-permute-start(bf16[2,64,640]{2,1,0:T(8,128)(2,1)S(1)} %collective-permute-done.11.refs_2_), channel_id=1, source_target_pairs={{0,2},{2,0},{4,6},{6,4},{8,10},{10,8},{12,14},{14,12},{1,3},{3,1},... | collective-permute-start | bytes 491528 | tf_op jit(solution)/shard_map/ppermute | solution.py:249
  57.4 4.8 %collective-permute-start.14 = (bf16[2,64,640]{2,1,0:T(8,128)(2,1)S(1)}, bf16[2,64,640]{2,1,0:T(8,128)(2,1)S(1)}, u32[]{:S(2)}, u32[]{:S(2)}) collective-permute-start(bf16[2,64,640]{2,1,0:T(8,128)(2,1)S(1)} %collective-permute-done.10.refs_1_), channel_id=1, source_target_pairs={{0,2},{2,0},{4,6},{6,4},{8,10},{10,8},{12,14},{14,12},{1,3},{3,1},... | collective-permute-start | bytes 491528 | tf_op jit(solution)/shard_map/ppermute | solution.py:249
  58.9 7.1 %collective-permute-start.24 = (bf16[640,128]{1,0:T(8,128)(2,1)S(1)}, bf16[640,128]{1,0:T(8,128)(2,1)S(1)}, u32[]{:S(2)}, u32[]{:S(2)}) collective-permute-start(bf16[640,128]{1,0:T(8,128)(2,1)S(1)} %project.3), channel_id=1, source_target_pairs={{0,1},{1,0},{2,3},{3,2},{4,5},{5,4},{6,7},{7,6},{8,9},{9,8},{10,11... | collective-permute-start | bytes 491528 | tf_op jit(solution)/shard_map/ppermute | solution.py:246
  61.4 7.3 %collective-permute-start.27 = (bf16[640,128]{1,0:T(8,128)(2,1)S(1)}, bf16[640,128]{1,0:T(8,128)(2,1)S(1)}, u32[]{:S(2)}, u32[]{:S(2)}) collective-permute-start(bf16[640,128]{1,0:T(8,128)(2,1)S(1)} %project.4), channel_id=1, source_target_pairs={{0,1},{1,0},{2,3},{3,2},{4,5},{5,4},{6,7},{7,6},{8,9},{9,8},{10,11... | collective-permute-start | bytes 491528 | tf_op jit(solution)/shard_map/ppermute | solution.py:246
where the time goes:
time: 70.8 us; the launch traced here: 70.6 us
  waiting for transfers between devices  29.7 us (42%)
  starting transfers between devices  26.4 us (37%)
  Pallas kernels  9.31 us (13%)
  other arithmetic  3.61 us (5%)
  between operations  1.46 us (2%)
    ppermute x1, waiting for transfers between devices, head_sharded(): far = lax.ppermute(sent, 'blk', along(2))  9.72 us
    ppermute x2, waiting for transfers between devices, head_sharded(): received.append(lax.ppermute(partial, 'heads', across))  6.49 us
    ppermute x3, starting transfers between devices, head_sharded(): lax.ppermute(keyed[j], 'blk', along(j))  5.71 us
    ppermute x3, waiting for transfers between devices, head_sharded(): lax.ppermute(asked[j], 'blk', along(j))  4.93 us
    ppermute x3, starting transfers between devices, head_sharded(): lax.ppermute(asked[j], 'blk', along(j))  4.45 us
    ppermute x3, starting transfers between devices, head_sharded(): pieces = [kept] + [lax.ppermute(kept, 'blk', along(j)) for j in (1, 2, 3)]  4.45 us
    ppermute x2, waiting for transfers between devices, head_sharded(): relayed = lax.ppermute(far[n:n + 1], 'blk', along(1))  4.27 us
    ppermute x2, starting transfers between devices, head_sharded(): relayed = lax.ppermute(far[n:n + 1], 'blk', along(1))  4.04 us
  transfers between devices with their start and end apart: 28, of which 9 were waited for; matrix products, arithmetic and copies ran while one was open for 5% of the time, Pallas kernels for 5%

commit v1 on v0

--- a/solution.py
+++ b/solution.py
@@ -3,7 +3,6 @@
 
 import jax
 import jax.numpy as jnp
-import numpy as np
 from jax import lax
 from jax.experimental import pallas as pl
 from jax.experimental.pallas import tpu as pltpu
@@ -24,6 +23,10 @@
 
 def room(mib):
     return pltpu.CompilerParams(vmem_limit_bytes=mib * 1024 * 1024)
+
+
+KROOM = 54950
+QROOM = 54800
 
 
 def pack_kernel(chips, groups, *refs):
@@ -58,7 +61,7 @@
         copy.wait()
 
 
-def pack(chips, *groups):
+def pack(kib, chips, *groups):
     slabs = [(group[0].shape[0], sum(x.shape[1] for x in group) // chips) for group in groups]
     out = pl.pallas_call(
         functools.partial(pack_kernel, chips, [len(group) for group in groups]),
@@ -68,7 +71,7 @@
         scratch_shapes=[pltpu.VMEM((chips, *slab), jnp.bfloat16) for slab in slabs]
         + [pltpu.SemaphoreType.DMA((chips, len(group))) for group in groups]
         + [pltpu.SemaphoreType.DMA((chips,)) for _ in groups],
-        name="pack",
+        compiler_params=pltpu.CompilerParams(vmem_limit_bytes=kib * 1024),
     )(*(x for group in groups for x in group))
     return [out[g * chips : (g + 1) * chips] for g in range(len(groups))]
 
@@ -151,28 +154,51 @@
         pl.when(half == value)(functools.partial(attend, blocks))
 
 
-def project_kernel(picks, w_ref, *refs):
-    pieces = len(picks)
-    own, other, added = refs[:pieces], refs[pieces : 2 * pieces], refs[2 * pieces : -2]
-    out_ref, rows_s = refs[-2:]
+def project_kernel(distances, final, column, w_ref, *refs):
+    pieces = len(distances)
+    own, other, added = refs[:pieces], refs[pieces : 2 * pieces], refs[2 * pieces :]
+    added, scratch = (added[:-4], added[-4:]) if final else (added[:-2], added[-2:])
+    out_ref, rows_s = scratch[:2]
     me = lax.axis_index("blk")
     chip, core = me // CORES, me % CORES
-    rows, width = own[0].shape[1:]
-    for j, blocks in enumerate(picks):
-        at = pl.multiple_of((chip ^ j) * width, HEAD_SIZE)
+    blocks, rows, width = own[0].shape
+    apart = pieces < w_ref.shape[1] // width
+    for j in range(pieces):
+        at = 0 if apart else pl.multiple_of((chip ^ distances[j]) * width, HEAD_SIZE)
         for piece, side in ((own[j], core), (other[j], 1 - core)):
-            for n, block in enumerate(blocks):
+            for n in range(blocks):
                 to = pl.multiple_of((n * CORES + side) * rows, rows)
-                rows_s[pl.ds(to, rows), pl.ds(at, width)] = piece[block]
-    product = lax.dot_general(
-        w_ref[...], rows_s[...], (((1,), (1,)), ((), ())), preferred_element_type=jnp.float32
-    )
-    if not added:
-        out_ref[...] = product.astype(jnp.bfloat16)
-    for n, ref in enumerate(added):
-        count = ref.shape[1]
-        lanes = slice(n * count, (n + 1) * count)
-        out_ref[:, lanes] = (product[:, lanes] + ref[...].astype(jnp.float32)).astype(jnp.bfloat16)
+                rows_s[j if apart else 0, pl.ds(to, rows), pl.ds(at, width)] = piece[n]
+
+    def dot(a, b):
+        return lax.dot_general(a, b, (((1,), (1,)), ((), ())), preferred_element_type=jnp.float32)
+
+    def share(lines):
+        if apart:
+            total = None
+            for j, distance in enumerate(distances):
+                at = pl.multiple_of((chip ^ distance) * width, HEAD_SIZE)
+                product = dot(w_ref[lines, pl.ds(at, width)], rows_s[j])
+                total = product if total is None else total + product
+        else:
+            total = dot(w_ref[lines], rows_s[0])
+        for ref in added:
+            total = total + ref[lines, column : column + total.shape[1]].astype(jnp.float32)
+        return total
+
+    features = w_ref.shape[0]
+    if not final:
+        out_ref[...] = share(slice(0, features)).astype(out_ref.dtype)
+        return
+    staged, sem = scratch[2:]
+    copies = []
+    for n in range(2):
+        lines = slice(n * features // 2, (n + 1) * features // 2)
+        staged[lines] = share(lines).astype(out_ref.dtype)
+        copies.append(pltpu.make_async_copy(staged.at[lines], out_ref.at[lines], sem.at[n]))
+        copies[-1].start()
+    for copy in copies:
+        copy.wait()
 
 
 def head_sharded(chips, span_q, span_k, span_values, cached_keys, cached_values, out_weight, ctx_len, span_start):
@@ -189,9 +215,10 @@
     partner = [(b, b ^ 1) for b in range(devices)]
     across = [(0, 1), (1, 0)]
 
-    keyed, asked = pack(chips, (span_k, span_values, cached_keys, cached_values), (span_q,))
+    keyed = pack(KROOM, chips, (span_k, span_values, cached_keys, cached_values))[0]
+    asked = pack(QROOM, chips, (span_q,))[0]
     half_dim = HEAD_SIZE // 2
-    inverse = jnp.asarray(np.float32(ROPE_BASE) ** (-(np.arange(half_dim, dtype=np.float32) * 2.0 / HEAD_SIZE)))
+    inverse = ROPE_BASE ** (-(jnp.arange(half_dim, dtype=jnp.float32) * 2.0 / HEAD_SIZE))
     positions = span_start[0] + jnp.arange(total_rows, dtype=jnp.int32)
     angles = positions.astype(jnp.float32)[:, None] * inverse[None, :]
     cosine, sine = jnp.cos(angles), jnp.sin(angles)
@@ -201,9 +228,8 @@
     keys = [keyed[0]] + [lax.ppermute(keyed[j], "blk", along(j)) for j in range(1, chips)]
     queries = [asked[0]] + [lax.ppermute(asked[j], "blk", along(j)) for j in range(1, chips)]
     keys[1], cosine, sine = lax.optimization_barrier((keys[1], cosine, sine))
+    keys[0], cosine, sine = lax.optimization_barrier((keys[0], cosine, sine))
     swapped = [lax.ppermute(x, "blk", partner) for x in keys]
-    here = ctx_len[0] >= 0
-    keys[0], queries[0] = (jnp.where(here, x, jnp.zeros_like(x)) for x in (keys[0], queries[0]))
     half_chips = chips // 2
 
     def attend(own_half):
@@ -219,35 +245,44 @@
             cost_estimate=pl.CostEstimate(flops=400_000_000, bytes_accessed=1_000_000, transcendentals=600_000),
         )(*queries, *keys, *swapped, cosine, sine, ctx_len)
 
-    def project(picks, pieces, others, *added):
-        count = len(picks[0]) * CORES * rows
+
+    def project(distances, pieces, others, *added, dtype=jnp.bfloat16, final=False, column=0):
+        count = pieces[0].shape[0] * CORES * rows
+        apart = len(pieces) < chips
+        scratch = [pltpu.VMEM((len(pieces), count, width) if apart else (1, count, chips * width), jnp.bfloat16)]
+        if final:
+            scratch += [pltpu.VMEM((features, count), dtype), pltpu.SemaphoreType.DMA((2,))]
         return pl.pallas_call(
-            functools.partial(project_kernel, picks),
-            out_shape=jax.ShapeDtypeStruct((features, count), jnp.bfloat16),
+            functools.partial(project_kernel, distances, final, column),
+            out_shape=jax.ShapeDtypeStruct((features, count), dtype),
             in_specs=[whole()] * (1 + 2 * len(pieces) + len(added)),
-            out_specs=whole(),
-            scratch_shapes=[pltpu.VMEM((count, chips * width), jnp.bfloat16)],
+            out_specs=whole(pl.ANY if final else pltpu.VMEM),
+            scratch_shapes=scratch,
             name="project",
             compiler_params=room(12),
-            cost_estimate=pl.CostEstimate(flops=3_000_000 * count, bytes_accessed=8_000 * count, transcendentals=0),
+            cost_estimate=pl.CostEstimate(
+                flops=2 * features * width * count * len(pieces), bytes_accessed=1_000_000, transcendentals=0
+            ),
         )(out_weight, *pieces, *others, *added)
+
+    def swap(pieces):
+        return [lax.ppermute(piece, "blk", partner) for piece in pieces]
 
     sent = attend(False)
     far = lax.ppermute(sent, "blk", along(2))
     near = lax.ppermute(sent, "blk", along(1))
     pieces = [sent, near, far]
-    others = [lax.ppermute(piece, "blk", partner) for piece in pieces]
+    early = project((0, 1, 2), pieces, swap(pieces), dtype=jnp.float32)
     received = []
     for n in range(half_chips):
         relayed = lax.ppermute(far[n : n + 1], "blk", along(1))
         other = lax.ppermute(relayed, "blk", partner)
-        picks = ((n,), (n,), (n,), (0,))
-        partial = project(picks, [*pieces, relayed], [*others, other])
+        partial = project((3,), [relayed], [other], early, column=n * CORES * rows)
         received.append(lax.ppermute(partial, "heads", across))
     kept = attend(True)
     pieces = [kept] + [lax.ppermute(kept, "blk", along(j)) for j in (1, 2, 3)]
-    others = [lax.ppermute(piece, "blk", partner) for piece in pieces]
-    return project((tuple(range(half_chips)),) * chips, pieces, others, *received)
+    others = swap(pieces)
+    return project((0, 1, 2, 3), pieces, others, jnp.concatenate(received, axis=1), final=True)
 
 
 def rotary(inputs, positions):

time: 70.8 us -> 60.8 us (0.86)
  waiting for transfers between devices: 29.7 us -> 25.4 us
  starting transfers between devices: 26.4 us -> 22.8 us
  other arithmetic: 3.61 us -> 1.25 us
    ppermute x1, waiting for transfers between devices: 9.72 us -> 2.02 us  [head_sharded(): far = lax.ppermute(sent, 'blk', along(2))]
    ppermute x2, waiting for transfers between devices: 6.49 us -> 0.01 us  [head_sharded(): received.append(lax.ppermute(partial, 'heads', across))]
    ppermute x3, waiting for transfers between devices: 2.02 us -> 8.36 us  [head_sharded(): pieces = [kept] + [lax.ppermute(kept, 'blk', along(j)) for j in (1, 2, 3)]]
    ppermute x1, waiting for transfers between devices: 2.25 us -> 5.77 us  [head_sharded(): near = lax.ppermute(sent, 'blk', along(1))]
    ppermute x2, starting transfers between devices: 4.04 us -> 2.09 us  [head_sharded(): relayed = lax.ppermute(far[n:n + 1], 'blk', along(1))]
    select_n x2 -> x0, other arithmetic: 1.75 us -> none  [head_sharded(): jnp.where(here, x, jnp.zeros_like(x))]
    ppermute x7, waiting for transfers between devices: 0.02 us -> 1.28 us  [swap(): return [lax.ppermute(piece, 'blk', partner) for piece in pieces]]
    ppermute x7, starting transfers between devices: 1.59 us -> 0.59 us  [swap(): return [lax.ppermute(piece, 'blk', partner) for piece in pieces]]
  transfers between devices with their start and end apart: 28 -> 28, of which waited for: 9 -> 10; matrix products, arithmetic and copies ran while one was open for 5% -> 2% of each run, Pallas kernels for 5% -> 8%
where the time goes in v1:
time: 60.8 us; the launch traced here: 60.6 us
  waiting for transfers between devices  25.4 us (42%)
  starting transfers between devices  22.8 us (38%)
  Pallas kernels  9.62 us (16%)
  between operations  1.5 us (2%)
  other arithmetic  1.25 us (2%)
    ppermute x3, waiting for transfers between devices, head_sharded(): pieces = [kept] + [lax.ppermute(kept, 'blk', along(j)) for j in (1, 2, 3)]  8.36 us
    ppermute x1, waiting for transfers between devices, head_sharded(): near = lax.ppermute(sent, 'blk', along(1))  5.77 us
    ppermute x3, starting transfers between devices, head_sharded(): lax.ppermute(keyed[j], 'blk', along(j))  5.71 us
    ppermute x3, waiting for transfers between devices, head_sharded(): lax.ppermute(asked[j], 'blk', along(j))  4.68 us
    ppermute x3, starting transfers between devices, head_sharded(): lax.ppermute(asked[j], 'blk', along(j))  4.52 us
    ppermute x3, starting transfers between devices, head_sharded(): pieces = [kept] + [lax.ppermute(kept, 'blk', along(j)) for j in (1, 2, 3)]  4.45 us
    pallas_call x4, Pallas kernels, project(): pl.pallas_call(functools.partial(project_kernel, distances, final, column...  3.73 us
    ppermute x2, waiting for transfers between devices, head_sharded(): relayed = lax.ppermute(far[n:n + 1], 'blk', along(1))  3.29 us
  transfers between devices with their start and end apart: 28, of which 10 were waited for; matrix products, arithmetic and copies ran while one was open for 2% of the time, Pallas kernels for 8%

profile of v1, /device:TPU:0, one launch (start us, length us, event | category | flops | bytes accessed | tf_op | source)
XLA Modules:
  0.0 60.6 jit_solution(11454614892035002387)
XLA Ops:
  0.0 1.4 %shard_map.83 = (bf16[64,512]{1,0:T(8,128)(2,1)S(1)}, bf16[64,512]{1,0:T(8,128)(2,1)S(1)}, bf16[64,512]{1,0:T(8,128)(2,1)S(1)}, bf16[64,512]{1,0:T(8,128)(2,1)S(1)}) custom-call(bf16[64,512]{1,0:T(8,128)(2,1)} %refs_0_.3, bf16[64,512]{1,0:T(8,128)(2,1)} %refs_1_.1, bf16[64,512]{1,0:T(8,128)(2,1)} %refs_2_.1, bf16[64,512]{1,0:T(8,128)(2,1)} %refs_3_.1), custom_call_target="tpu_custom_call" | custom-call | tf_op jit(solution)/shard_map/pallas_call | solution.py:66
  1.5 3.1 %collective-permute-start.3 = (bf16[64,512]{1,0:T(8,128)(2,1)S(1)}, bf16[64,512]{1,0:T(8,128)(2,1)S(1)}, u32[]{:S(2)}, u32[]{:S(2)}) collective-permute-start(bf16[64,512]{1,0:T(8,128)(2,1)S(1)} %get-tuple-element.24), channel_id=1, source_target_pairs={{0,4},{2,6},{4,0},{6,2},{8,12},{10,14},{12,8},{14,10},{1,5},{3,7},... | collective-permute-start | bytes 196616 | tf_op jit(solution)/shard_map/ppermute | solution.py:228
  4.6 2.6 %collective-permute-start.4 = (bf16[64,512]{1,0:T(8,128)(2,1)S(1)}, bf16[64,512]{1,0:T(8,128)(2,1)S(1)}, u32[]{:S(2)}, u32[]{:S(2)}) collective-permute-start(bf16[64,512]{1,0:T(8,128)(2,1)S(1)} %get-tuple-element.29), channel_id=1, source_target_pairs={{0,8},{2,10},{4,12},{6,14},{8,0},{10,2},{12,4},{14,6},{1,9},{3,11}... | collective-permute-start | bytes 196616 | tf_op jit(solution)/shard_map/ppermute | solution.py:228
  7.2 1.3 %shard_map.82 = (bf16[64,640]{1,0:T(8,128)(2,1)S(1)}, bf16[64,640]{1,0:T(8,128)(2,1)S(1)}, bf16[64,640]{1,0:T(8,128)(2,1)S(1)}, bf16[64,640]{1,0:T(8,128)(2,1)S(1)}) custom-call(bf16[64,2560]{1,0:T(8,128)(2,1)} %refs_0_.2), custom_call_target="tpu_custom_call" | custom-call | tf_op jit(solution)/shard_map/pallas_call | solution.py:66
  8.5 1.0 %collective-permute-start = (bf16[64,640]{1,0:T(8,128)(2,1)S(1)}, bf16[64,640]{1,0:T(8,128)(2,1)S(1)}, u32[]{:S(2)}, u32[]{:S(2)}) collective-permute-start(bf16[64,640]{1,0:T(8,128)(2,1)S(1)} %get-tuple-element.20), channel_id=1, source_target_pairs={{0,4},{2,6},{4,0},{6,2},{8,12},{10,14},{12,8},{14,10},{1,5},{3,7},... | collective-permute-start | bytes 245768 | tf_op jit(solution)/shard_map/ppermute | solution.py:229
  9.5 3.5 %collective-permute-start.1 = (bf16[64,640]{1,0:T(8,128)(2,1)S(1)}, bf16[64,640]{1,0:T(8,128)(2,1)S(1)}, u32[]{:S(2)}, u32[]{:S(2)}) collective-permute-start(bf16[64,640]{1,0:T(8,128)(2,1)S(1)} %get-tuple-element.21), channel_id=1, source_target_pairs={{0,8},{2,10},{4,12},{6,14},{8,0},{10,2},{12,4},{14,6},{1,9},{3,11}... | collective-permute-start | bytes 245768 | tf_op jit(solution)/shard_map/ppermute | solution.py:229
  13.7 1.0 %fusion = (f32[512,64]{1,0:T(8,128)S(1)}, f32[512,64]{1,0:T(8,128)S(1)}, f32[512,64]{1,0:T(8,128)S(1)}) fusion(f32[64]{0:T(128)S(1)} %negate_power_fusion, f32[512]{0:T(512)S(1)} %add_convert_fusion), kind=kLoop, calls=%fused_computation.5 | loop fusion | flops 65536 | bytes 395520 | tf_op jit(solution)/shard_map/neg | solution.py:226
  14.7 0.0 collective-permute-done.3.refs_5_
  14.7 0.1 collective-permute-start.2
  14.7 0.2 pad_maximum_fusion.1
  14.9 0.0 collective-permute-done.4.refs_6_
  15.0 0.1 collective-permute-start.6
  15.0 0.5 collective-permute-start.8
  15.5 0.1 collective-permute-start.9
  15.6 1.5 %collective-permute-done.1.refs_2_ = bf16[64,640]{1,0:T(8,128)(2,1)S(1)} collective-permute-done((bf16[64,640]{1,0:T(8,128)(2,1)S(1)}, bf16[64,640]{1,0:T(8,128)(2,1)S(1)}, u32[]{:S(2)}, u32[]{:S(2)}) %collective-permute-start.1) | collective-permute-done | bytes 81952 | tf_op jit(solution)/shard_map/ppermute | solution.py:229
  17.2 0.0 collective-permute-start.7
  17.8 3.2 %collective-permute-done.2.refs_3_ = bf16[64,640]{1,0:T(8,128)(2,1)S(1)} collective-permute-done((bf16[64,640]{1,0:T(8,128)(2,1)S(1)}, bf16[64,640]{1,0:T(8,128)(2,1)S(1)}, u32[]{:S(2)}, u32[]{:S(2)}) %collective-permute-start.2) | collective-permute-done | bytes 81952 | tf_op jit(solution)/shard_map/ppermute | solution.py:229
  21.0 0.0 collective-permute-done.8.refs_10_
  21.0 0.0 collective-permute-done.9.refs_11_
  21.0 0.0 collective-permute-done.6.refs_8_
  21.0 1.6 %attend.3.refs_0_ = bf16[2,64,640]{2,1,0:T(8,128)(2,1)S(1)} custom-call(bf16[64,640]{1,0:T(8,128)(2,1)S(1)} %get-tuple-element.19.refs_0_, bf16[64,640]{1,0:T(8,128)(2,1)S(1)} %collective-permute-done.refs_1_, bf16[64,640]{1,0:T(8,128)(2,1)S(1)} %collective-permute-done.1.refs_2_, bf16[64,640]{1,0:T(8,128)(2,1)S(1)} %collective-permute-done.2.refs_3_, ...), custom_call_target="tpu_custom_call" | custom-call | flops 400000000 | bytes 1000000 | tf_op jit(solution)/shard_map/attend/pallas_call | solution.py:236
  22.6 0.1 collective-permute-start.20
  22.7 2.5 %collective-permute-start.17 = (bf16[2,64,640]{2,1,0:T(8,128)(2,1)S(1)}, bf16[2,64,640]{2,1,0:T(8,128)(2,1)S(1)}, u32[]{:S(2)}, u32[]{:S(2)}) collective-permute-start(bf16[2,64,640]{2,1,0:T(8,128)(2,1)S(1)} %attend.3.refs_0_), channel_id=1, source_target_pairs={{0,8},{2,10},{4,12},{6,14},{8,0},{10,2},{12,4},{14,6},{1,9},{3,11}... | collective-permute-start | bytes 491528 | tf_op jit(solution)/shard_map/ppermute | solution.py:272
  25.3 5.8 %collective-permute-done.20.refs_1_ = bf16[2,64,640]{2,1,0:T(8,128)(2,1)S(1)} collective-permute-done((bf16[2,64,640]{2,1,0:T(8,128)(2,1)S(1)}, bf16[2,64,640]{2,1,0:T(8,128)(2,1)S(1)}, u32[]{:S(2)}, u32[]{:S(2)}) %collective-permute-start.20) | collective-permute-done | bytes 163872 | tf_op jit(solution)/shard_map/ppermute | solution.py:273
  31.0 2.0 %collective-permute-done.17.refs_2_ = bf16[2,64,640]{2,1,0:T(8,128)(2,1)S(1)} collective-permute-done((bf16[2,64,640]{2,1,0:T(8,128)(2,1)S(1)}, bf16[2,64,640]{2,1,0:T(8,128)(2,1)S(1)}, u32[]{:S(2)}, u32[]{:S(2)}) %collective-permute-start.17) | collective-permute-done | bytes 163872 | tf_op jit(solution)/shard_map/ppermute | solution.py:272
  33.1 0.4 collective-permute-start.18
  33.5 1.7 %collective-permute-start.25 = (bf16[1,64,640]{2,1,0:T(8,128)(2,1)S(1)}, bf16[1,64,640]{2,1,0:T(8,128)(2,1)S(1)}, u32[]{:S(2)}, u32[]{:S(2)}) collective-permute-start(bf16[1,64,640]{2,1,0:T(8,128)(2,1)S(1)} %get-tuple-element.34), channel_id=1, source_target_pairs={{0,4},{2,6},{4,0},{6,2},{8,12},{10,14},{12,8},{14,10},{1,5},{3,7},... | collective-permute-start | bytes 245768 | tf_op jit(solution)/shard_map/ppermute | solution.py:278
  35.2 3.3 %collective-permute-done.18.refs_0_ = bf16[1,64,640]{2,1,0:T(8,128)(2,1)S(1)} collective-permute-done((bf16[1,64,640]{2,1,0:T(8,128)(2,1)S(1)}, bf16[1,64,640]{2,1,0:T(8,128)(2,1)S(1)}, u32[]{:S(2)}, u32[]{:S(2)}) %collective-permute-start.18) | collective-permute-done | bytes 81952 | tf_op jit(solution)/shard_map/ppermute | solution.py:278
  38.5 0.0 collective-permute-start.19
  38.5 1.4 %attend.2.refs_0_ = bf16[2,64,640]{2,1,0:T(8,128)(2,1)S(1)} custom-call(bf16[64,640]{1,0:T(8,128)(2,1)S(1)} %get-tuple-element.19.refs_0_, bf16[64,640]{1,0:T(8,128)(2,1)S(1)} %collective-permute-done.refs_1_, bf16[64,640]{1,0:T(8,128)(2,1)S(1)} %collective-permute-done.1.refs_2_, bf16[64,640]{1,0:T(8,128)(2,1)S(1)} %collective-permute-done.2.refs_3_, ...), custom_call_target="tpu_custom_call" | custom-call | flops 400000000 | bytes 1000000 | tf_op jit(solution)/shard_map/attend/pallas_call | solution.py:236
  39.9 2.5 %collective-permute-start.12 = (bf16[2,64,640]{2,1,0:T(8,128)(2,1)S(1)}, bf16[2,64,640]{2,1,0:T(8,128)(2,1)S(1)}, u32[]{:S(2)}, u32[]{:S(2)}) collective-permute-start(bf16[2,64,640]{2,1,0:T(8,128)(2,1)S(1)} %attend.2.refs_0_), channel_id=1, source_target_pairs={{0,12},{2,14},{4,8},{6,10},{8,4},{10,6},{12,0},{14,2},{1,13},{3,15... | collective-permute-start | bytes 491528 | tf_op jit(solution)/shard_map/ppermute | solution.py:283
  42.4 0.0 collective-permute-done.25.refs_0_
  42.4 0.0 collective-permute-start.11
  42.4 0.0 collective-permute-done.22.refs_4_
  42.4 1.9 %collective-permute-start.10 = (bf16[2,64,640]{2,1,0:T(8,128)(2,1)S(1)}, bf16[2,64,640]{2,1,0:T(8,128)(2,1)S(1)}, u32[]{:S(2)}, u32[]{:S(2)}) collective-permute-start(bf16[2,64,640]{2,1,0:T(8,128)(2,1)S(1)} %attend.2.refs_0_), channel_id=1, source_target_pairs={{0,4},{2,6},{4,0},{6,2},{8,12},{10,14},{12,8},{14,10},{1,5},{3,7},... | collective-permute-start | bytes 491528 | tf_op jit(solution)/shard_map/ppermute | solution.py:283
  44.4 1.0 %project.4.refs_2_ = f32[640,256]{1,0:T(8,128)S(1)} custom-call(bf16[640,2560]{1,0:T(8,128)(2,1)S(1)} %copy-done, bf16[2,64,640]{2,1,0:T(8,128)(2,1)S(1)} %attend.3.refs_0_, bf16[2,64,640]{2,1,0:T(8,128)(2,1)S(1)} %collective-permute-done.20.refs_1_, bf16[2,64,640]{2,1,0:T(8,128)(2,1)S(1)} %collective-permute-done.17.refs_2_, ...), custom_call_target="tpu_custom_call" | custom-call | flops 629145600 | bytes 1000000 | tf_op jit(solution)/shard_map/project/pallas_call | solution.py:255
  45.5 0.4 project.5
  45.9 1.5 %collective-permute-start.24 = (bf16[640,128]{1,0:T(8,128)(2,1)S(1)}, bf16[640,128]{1,0:T(8,128)(2,1)S(1)}, u32[]{:S(2)}, u32[]{:S(2)}) collective-permute-start(bf16[640,128]{1,0:T(8,128)(2,1)S(1)} %project.5), channel_id=1, source_target_pairs={{0,1},{1,0},{2,3},{3,2},{4,5},{5,4},{6,7},{7,6},{8,9},{9,8},{10,11... | collective-permute-start | bytes 491528 | tf_op jit(solution)/shard_map/ppermute | solution.py:281
  47.4 0.4 project.6
  47.8 0.6 %collective-permute-start.27 = (bf16[640,128]{1,0:T(8,128)(2,1)S(1)}, bf16[640,128]{1,0:T(8,128)(2,1)S(1)}, u32[]{:S(2)}, u32[]{:S(2)}) collective-permute-start(bf16[640,128]{1,0:T(8,128)(2,1)S(1)} %project.6), channel_id=1, source_target_pairs={{0,1},{1,0},{2,3},{3,2},{4,5},{5,4},{6,7},{7,6},{8,9},{9,8},{10,11... | collective-permute-start | bytes 491528 | tf_op jit(solution)/shard_map/ppermute | solution.py:281
  48.4 0.6 collective-permute-done.12.refs_3_
  49.0 7.8 %collective-permute-done.11.refs_2_ = bf16[2,64,640]{2,1,0:T(8,128)(2,1)S(1)} collective-permute-done((bf16[2,64,640]{2,1,0:T(8,128)(2,1)S(1)}, bf16[2,64,640]{2,1,0:T(8,128)(2,1)S(1)}, u32[]{:S(2)}, u32[]{:S(2)}) %collective-permute-start.11) | collective-permute-done | bytes 163872 | tf_op jit(solution)/shard_map/ppermute | solution.py:283
  56.8 0.5 collective-permute-start.15
  57.3 0.1 collective-permute-start.14
  57.4 0.8 %collective-permute-done.16.refs_7_ = bf16[2,64,640]{2,1,0:T(8,128)(2,1)S(1)} collective-permute-done((bf16[2,64,640]{2,1,0:T(8,128)(2,1)S(1)}, bf16[2,64,640]{2,1,0:T(8,128)(2,1)S(1)}, u32[]{:S(2)}, u32[]{:S(2)}) %collective-permute-start.16) | collective-permute-done | bytes 163872 | tf_op jit(solution)/shard_map/ppermute | solution.py:269
  58.2 0.2 collective-permute-done.15.refs_6_
  58.4 0.3 collective-permute-done.14.refs_5_
  58.7 1.9 %project.7 = bf16[640,256]{1,0:T(8,128)(2,1)} custom-call(bf16[640,2560]{1,0:T(8,128)(2,1)S(1)} %copy-done, bf16[2,64,640]{2,1,0:T(8,128)(2,1)S(1)} %attend.2.refs_0_, bf16[2,64,640]{2,1,0:T(8,128)(2,1)S(1)} %collective-permute-done.10.refs_1_, bf16[2,64,640]{2,1,0:T(8,128)(2,1)S(1)} %collective-permute-done.11.refs_2_, ...), custom_call_target="tpu_custom_call" | custom-call | flops 838860800 | bytes 1000000 | tf_op jit(solution)/shard_map/project/pallas_call | solution.py:255
  (24 shorter events, 0.1 us)
Async XLA Ops:
  0.0 44.4 %copy-start = (bf16[640,2560]{1,0:T(8,128)(2,1)S(1)}, bf16[640,2560]{1,0:T(8,128)(2,1)}, u32[]{:S(2)}) copy-start(bf16[640,2560]{1,0:T(8,128)(2,1)} %w_ref.7) | copy-start | bytes 9830404
  1.5 13.2 %collective-permute-start.3 = (bf16[64,512]{1,0:T(8,128)(2,1)S(1)}, bf16[64,512]{1,0:T(8,128)(2,1)S(1)}, u32[]{:S(2)}, u32[]{:S(2)}) collective-permute-start(bf16[64,512]{1,0:T(8,128)(2,1)S(1)} %get-tuple-element.24), channel_id=1, source_target_pairs={{0,4},{2,6},{4,0},{6,2},{8,12},{10,14},{12,8},{14,10},{1,5},{3,7},... | collective-permute-start | bytes 196616 | tf_op jit(solution)/shard_map/ppermute | solution.py:228
  4.6 10.4 %collective-permute-start.4 = (bf16[64,512]{1,0:T(8,128)(2,1)S(1)}, bf16[64,512]{1,0:T(8,128)(2,1)S(1)}, u32[]{:S(2)}, u32[]{:S(2)}) collective-permute-start(bf16[64,512]{1,0:T(8,128)(2,1)S(1)} %get-tuple-element.29), channel_id=1, source_target_pairs={{0,8},{2,10},{4,12},{6,14},{8,0},{10,2},{12,4},{14,6},{1,9},{3,11}... | collective-permute-start | bytes 196616 | tf_op jit(solution)/shard_map/ppermute | solution.py:228
  7.2 7.9 %collective-permute-start.5 = (bf16[64,512]{1,0:T(8,128)(2,1)S(1)}, bf16[64,512]{1,0:T(8,128)(2,1)S(1)}, u32[]{:S(2)}, u32[]{:S(2)}) collective-permute-start(bf16[64,512]{1,0:T(8,128)(2,1)S(1)} %get-tuple-element.30), channel_id=1, source_target_pairs={{0,12},{2,14},{4,8},{6,10},{8,4},{10,6},{12,0},{14,2},{1,13},{3,15... | collective-permute-start | bytes 196616 | tf_op jit(solution)/shard_map/ppermute | solution.py:228
  8.5 7.0 %collective-permute-start = (bf16[64,640]{1,0:T(8,128)(2,1)S(1)}, bf16[64,640]{1,0:T(8,128)(2,1)S(1)}, u32[]{:S(2)}, u32[]{:S(2)}) collective-permute-start(bf16[64,640]{1,0:T(8,128)(2,1)S(1)} %get-tuple-element.20), channel_id=1, source_target_pairs={{0,4},{2,6},{4,0},{6,2},{8,12},{10,14},{12,8},{14,10},{1,5},{3,7},... | collective-permute-start | bytes 245768 | tf_op jit(solution)/shard_map/ppermute | solution.py:229
  9.5 7.7 %collective-permute-start.1 = (bf16[64,640]{1,0:T(8,128)(2,1)S(1)}, bf16[64,640]{1,0:T(8,128)(2,1)S(1)}, u32[]{:S(2)}, u32[]{:S(2)}) collective-permute-start(bf16[64,640]{1,0:T(8,128)(2,1)S(1)} %get-tuple-element.21), channel_id=1, source_target_pairs={{0,8},{2,10},{4,12},{6,14},{8,0},{10,2},{12,4},{14,6},{1,9},{3,11}... | collective-permute-start | bytes 245768 | tf_op jit(solution)/shard_map/ppermute | solution.py:229
  14.7 6.3 %collective-permute-start.2 = (bf16[64,640]{1,0:T(8,128)(2,1)S(1)}, bf16[64,640]{1,0:T(8,128)(2,1)S(1)}, u32[]{:S(2)}, u32[]{:S(2)}) collective-permute-start(bf16[64,640]{1,0:T(8,128)(2,1)S(1)} %get-tuple-element.22), channel_id=1, source_target_pairs={{0,12},{2,14},{4,8},{6,10},{8,4},{10,6},{12,0},{14,2},{1,13},{3,15... | collective-permute-start | bytes 245768 | tf_op jit(solution)/shard_map/ppermute | solution.py:229
  15.0 6.0 %collective-permute-start.6 = (bf16[64,512]{1,0:T(8,128)(2,1)S(1)}, bf16[64,512]{1,0:T(8,128)(2,1)S(1)}, u32[]{:S(2)}, u32[]{:S(2)}) collective-permute-start(bf16[64,512]{1,0:T(8,128)(2,1)S(1)} %get-tuple-element.27.refs_4_), channel_id=1, source_target_pairs={{0,2},{2,0},{4,6},{6,4},{8,10},{10,8},{12,14},{14,12},{1,3},{3,1},... | collective-permute-start | bytes 196616 | tf_op jit(solution)/shard_map/ppermute | solution.py:232
  15.0 5.9 %collective-permute-start.8 = (bf16[64,512]{1,0:T(8,128)(2,1)S(1)}, bf16[64,512]{1,0:T(8,128)(2,1)S(1)}, u32[]{:S(2)}, u32[]{:S(2)}) collective-permute-start(bf16[64,512]{1,0:T(8,128)(2,1)S(1)} %collective-permute-done.4.refs_6_), channel_id=1, source_target_pairs={{0,2},{2,0},{4,6},{6,4},{8,10},{10,8},{12,14},{14,12},{1,3},{3,1},... | collective-permute-start | bytes 196616 | tf_op jit(solution)/shard_map/ppermute | solution.py:232
  15.5 5.4 %collective-permute-start.9 = (bf16[64,512]{1,0:T(8,128)(2,1)S(1)}, bf16[64,512]{1,0:T(8,128)(2,1)S(1)}, u32[]{:S(2)}, u32[]{:S(2)}) collective-permute-start(bf16[64,512]{1,0:T(8,128)(2,1)S(1)} %collective-permute-done.5.refs_7_), channel_id=1, source_target_pairs={{0,2},{2,0},{4,6},{6,4},{8,10},{10,8},{12,14},{14,12},{1,3},{3,1},... | collective-permute-start | bytes 196616 | tf_op jit(solution)/shard_map/ppermute | solution.py:232
  17.2 3.8 %collective-permute-start.7 = (bf16[64,512]{1,0:T(8,128)(2,1)S(1)}, bf16[64,512]{1,0:T(8,128)(2,1)S(1)}, u32[]{:S(2)}, u32[]{:S(2)}) collective-permute-start(bf16[64,512]{1,0:T(8,128)(2,1)S(1)} %collective-permute-done.3.refs_5_), channel_id=1, source_target_pairs={{0,2},{2,0},{4,6},{6,4},{8,10},{10,8},{12,14},{14,12},{1,3},{3,1},... | collective-permute-start | bytes 196616 | tf_op jit(solution)/shard_map/ppermute | solution.py:232
  22.6 8.4 %collective-permute-start.20 = (bf16[2,64,640]{2,1,0:T(8,128)(2,1)S(1)}, bf16[2,64,640]{2,1,0:T(8,128)(2,1)S(1)}, u32[]{:S(2)}, u32[]{:S(2)}) collective-permute-start(bf16[2,64,640]{2,1,0:T(8,128)(2,1)S(1)} %attend.3.refs_0_), channel_id=1, source_target_pairs={{0,4},{2,6},{4,0},{6,2},{8,12},{10,14},{12,8},{14,10},{1,5},{3,7},... | collective-permute-start | bytes 491528 | tf_op jit(solution)/shard_map/ppermute | solution.py:273
  22.7 10.3 %collective-permute-start.17 = (bf16[2,64,640]{2,1,0:T(8,128)(2,1)S(1)}, bf16[2,64,640]{2,1,0:T(8,128)(2,1)S(1)}, u32[]{:S(2)}, u32[]{:S(2)}) collective-permute-start(bf16[2,64,640]{2,1,0:T(8,128)(2,1)S(1)} %attend.3.refs_0_), channel_id=1, source_target_pairs={{0,8},{2,10},{4,12},{6,14},{8,0},{10,2},{12,4},{14,6},{1,9},{3,11}... | collective-permute-start | bytes 491528 | tf_op jit(solution)/shard_map/ppermute | solution.py:272
  25.3 14.7 %collective-permute-start.21 = (bf16[2,64,640]{2,1,0:T(8,128)(2,1)S(1)}, bf16[2,64,640]{2,1,0:T(8,128)(2,1)S(1)}, u32[]{:S(2)}, u32[]{:S(2)}) collective-permute-start(bf16[2,64,640]{2,1,0:T(8,128)(2,1)S(1)} %attend.3.refs_0_), channel_id=1, source_target_pairs={{0,2},{2,0},{4,6},{6,4},{8,10},{10,8},{12,14},{14,12},{1,3},{3,1},... | collective-permute-start | bytes 491528 | tf_op jit(solution)/shard_map/ppermute | solution.py:269
  31.0 11.4 %collective-permute-start.22 = (bf16[2,64,640]{2,1,0:T(8,128)(2,1)S(1)}, bf16[2,64,640]{2,1,0:T(8,128)(2,1)S(1)}, u32[]{:S(2)}, u32[]{:S(2)}) collective-permute-start(bf16[2,64,640]{2,1,0:T(8,128)(2,1)S(1)} %collective-permute-done.20.refs_1_), channel_id=1, source_target_pairs={{0,2},{2,0},{4,6},{6,4},{8,10},{10,8},{12,14},{14,12},{1,3},{3,1},... | collective-permute-start | bytes 491528 | tf_op jit(solution)/shard_map/ppermute | solution.py:269
  33.1 11.3 %collective-permute-start.23 = (bf16[2,64,640]{2,1,0:T(8,128)(2,1)S(1)}, bf16[2,64,640]{2,1,0:T(8,128)(2,1)S(1)}, u32[]{:S(2)}, u32[]{:S(2)}) collective-permute-start(bf16[2,64,640]{2,1,0:T(8,128)(2,1)S(1)} %collective-permute-done.17.refs_2_), channel_id=1, source_target_pairs={{0,2},{2,0},{4,6},{6,4},{8,10},{10,8},{12,14},{14,12},{1,3},{3,1},... | collective-permute-start | bytes 491528 | tf_op jit(solution)/shard_map/ppermute | solution.py:269
  33.1 5.4 %collective-permute-start.18 = (bf16[1,64,640]{2,1,0:T(8,128)(2,1)S(1)}, bf16[1,64,640]{2,1,0:T(8,128)(2,1)S(1)}, u32[]{:S(2)}, u32[]{:S(2)}) collective-permute-start(bf16[1,64,640]{2,1,0:T(8,128)(2,1)S(1)} %get-tuple-element.33), channel_id=1, source_target_pairs={{0,4},{2,6},{4,0},{6,2},{8,12},{10,14},{12,8},{14,10},{1,5},{3,7},... | collective-permute-start | bytes 245768 | tf_op jit(solution)/shard_map/ppermute | solution.py:278
  33.5 9.0 %collective-permute-start.25 = (bf16[1,64,640]{2,1,0:T(8,128)(2,1)S(1)}, bf16[1,64,640]{2,1,0:T(8,128)(2,1)S(1)}, u32[]{:S(2)}, u32[]{:S(2)}) collective-permute-start(bf16[1,64,640]{2,1,0:T(8,128)(2,1)S(1)} %get-tuple-element.34), channel_id=1, source_target_pairs={{0,4},{2,6},{4,0},{6,2},{8,12},{10,14},{12,8},{14,10},{1,5},{3,7},... | collective-permute-start | bytes 245768 | tf_op jit(solution)/shard_map/ppermute | solution.py:278
  38.5 7.0 %collective-permute-start.19 = (bf16[1,64,640]{2,1,0:T(8,128)(2,1)S(1)}, bf16[1,64,640]{2,1,0:T(8,128)(2,1)S(1)}, u32[]{:S(2)}, u32[]{:S(2)}) collective-permute-start(bf16[1,64,640]{2,1,0:T(8,128)(2,1)S(1)} %collective-permute-done.18.refs_0_), channel_id=1, source_target_pairs={{0,2},{2,0},{4,6},{6,4},{8,10},{10,8},{12,14},{14,12},{1,3},{3,1},... | collective-permute-start | bytes 245768 | tf_op jit(solution)/shard_map/ppermute | solution.py:279
  39.9 9.1 %collective-permute-start.12 = (bf16[2,64,640]{2,1,0:T(8,128)(2,1)S(1)}, bf16[2,64,640]{2,1,0:T(8,128)(2,1)S(1)}, u32[]{:S(2)}, u32[]{:S(2)}) collective-permute-start(bf16[2,64,640]{2,1,0:T(8,128)(2,1)S(1)} %attend.2.refs_0_), channel_id=1, source_target_pairs={{0,12},{2,14},{4,8},{6,10},{8,4},{10,6},{12,0},{14,2},{1,13},{3,15... | collective-permute-start | bytes 491528 | tf_op jit(solution)/shard_map/ppermute | solution.py:283
  42.4 14.4 %collective-permute-start.11 = (bf16[2,64,640]{2,1,0:T(8,128)(2,1)S(1)}, bf16[2,64,640]{2,1,0:T(8,128)(2,1)S(1)}, u32[]{:S(2)}, u32[]{:S(2)}) collective-permute-start(bf16[2,64,640]{2,1,0:T(8,128)(2,1)S(1)} %attend.2.refs_0_), channel_id=1, source_target_pairs={{0,8},{2,10},{4,12},{6,14},{8,0},{10,2},{12,4},{14,6},{1,9},{3,11}... | collective-permute-start | bytes 491528 | tf_op jit(solution)/shard_map/ppermute | solution.py:283
  42.4 14.4 %collective-permute-start.10 = (bf16[2,64,640]{2,1,0:T(8,128)(2,1)S(1)}, bf16[2,64,640]{2,1,0:T(8,128)(2,1)S(1)}, u32[]{:S(2)}, u32[]{:S(2)}) collective-permute-start(bf16[2,64,640]{2,1,0:T(8,128)(2,1)S(1)} %attend.2.refs_0_), channel_id=1, source_target_pairs={{0,4},{2,6},{4,0},{6,2},{8,12},{10,14},{12,8},{14,10},{1,5},{3,7},... | collective-permute-start | bytes 491528 | tf_op jit(solution)/shard_map/ppermute | solution.py:283
  44.4 3.0 %collective-permute-start.26 = (bf16[1,64,640]{2,1,0:T(8,128)(2,1)S(1)}, bf16[1,64,640]{2,1,0:T(8,128)(2,1)S(1)}, u32[]{:S(2)}, u32[]{:S(2)}) collective-permute-start(bf16[1,64,640]{2,1,0:T(8,128)(2,1)S(1)} %collective-permute-done.25.refs_0_), channel_id=1, source_target_pairs={{0,2},{2,0},{4,6},{6,4},{8,10},{10,8},{12,14},{14,12},{1,3},{3,1},... | collective-permute-start | bytes 245768 | tf_op jit(solution)/shard_map/ppermute | solution.py:279
  45.9 11.4 %collective-permute-start.24 = (bf16[640,128]{1,0:T(8,128)(2,1)S(1)}, bf16[640,128]{1,0:T(8,128)(2,1)S(1)}, u32[]{:S(2)}, u32[]{:S(2)}) collective-permute-start(bf16[640,128]{1,0:T(8,128)(2,1)S(1)} %project.5), channel_id=1, source_target_pairs={{0,1},{1,0},{2,3},{3,2},{4,5},{5,4},{6,7},{7,6},{8,9},{9,8},{10,11... | collective-permute-start | bytes 491528 | tf_op jit(solution)/shard_map/ppermute | solution.py:281
  47.8 9.6 %collective-permute-start.27 = (bf16[640,128]{1,0:T(8,128)(2,1)S(1)}, bf16[640,128]{1,0:T(8,128)(2,1)S(1)}, u32[]{:S(2)}, u32[]{:S(2)}) collective-permute-start(bf16[640,128]{1,0:T(8,128)(2,1)S(1)} %project.6), channel_id=1, source_target_pairs={{0,1},{1,0},{2,3},{3,2},{4,5},{5,4},{6,7},{7,6},{8,9},{9,8},{10,11... | collective-permute-start | bytes 491528 | tf_op jit(solution)/shard_map/ppermute | solution.py:281
  49.0 8.4 %collective-permute-start.13 = (bf16[2,64,640]{2,1,0:T(8,128)(2,1)S(1)}, bf16[2,64,640]{2,1,0:T(8,128)(2,1)S(1)}, u32[]{:S(2)}, u32[]{:S(2)}) collective-permute-start(bf16[2,64,640]{2,1,0:T(8,128)(2,1)S(1)} %attend.2.refs_0_), channel_id=1, source_target_pairs={{0,2},{2,0},{4,6},{6,4},{8,10},{10,8},{12,14},{14,12},{1,3},{3,1},... | collective-permute-start | bytes 491528 | tf_op jit(solution)/shard_map/ppermute | solution.py:269
  56.8 1.4 %collective-permute-start.16 = (bf16[2,64,640]{2,1,0:T(8,128)(2,1)S(1)}, bf16[2,64,640]{2,1,0:T(8,128)(2,1)S(1)}, u32[]{:S(2)}, u32[]{:S(2)}) collective-permute-start(bf16[2,64,640]{2,1,0:T(8,128)(2,1)S(1)} %collective-permute-done.12.refs_3_), channel_id=1, source_target_pairs={{0,2},{2,0},{4,6},{6,4},{8,10},{10,8},{12,14},{14,12},{1,3},{3,1},... | collective-permute-start | bytes 491528 | tf_op jit(solution)/shard_map/ppermute | solution.py:269
  56.8 1.6 %collective-permute-start.15 = (bf16[2,64,640]{2,1,0:T(8,128)(2,1)S(1)}, bf16[2,64,640]{2,1,0:T(8,128)(2,1)S(1)}, u32[]{:S(2)}, u32[]{:S(2)}) collective-permute-start(bf16[2,64,640]{2,1,0:T(8,128)(2,1)S(1)} %collective-permute-done.11.refs_2_), channel_id=1, source_target_pairs={{0,2},{2,0},{4,6},{6,4},{8,10},{10,8},{12,14},{14,12},{1,3},{3,1},... | collective-permute-start | bytes 491528 | tf_op jit(solution)/shard_map/ppermute | solution.py:269
  57.3 1.4 %collective-permute-start.14 = (bf16[2,64,640]{2,1,0:T(8,128)(2,1)S(1)}, bf16[2,64,640]{2,1,0:T(8,128)(2,1)S(1)}, u32[]{:S(2)}, u32[]{:S(2)}) collective-permute-start(bf16[2,64,640]{2,1,0:T(8,128)(2,1)S(1)} %collective-permute-done.10.refs_1_), channel_id=1, source_target_pairs={{0,2},{2,0},{4,6},{6,4},{8,10},{10,8},{12,14},{14,12},{1,3},{3,1},... | collective-permute-start | bytes 491528 | tf_op jit(solution)/shard_map/ppermute | solution.py:269

commit v2 on v1

--- a/solution.py
+++ b/solution.py
@@ -76,37 +76,54 @@
     return [out[g * chips : (g + 1) * chips] for g in range(len(groups))]
 
 
-def attend_kernel(group, own_half, *refs):
-    slabs = (len(refs) - 9) // 3
-    queries, own, other = refs[:slabs], refs[slabs : 2 * slabs], refs[2 * slabs : 3 * slabs]
-    cos_ref, sin_ref, ctx_ref, out_ref, q_s, k_s, v_s, ck_s, cv_s = refs[3 * slabs :]
+def rotate(x, cosine, sine):
+    x = x.astype(jnp.float32)
+    turned = pltpu.roll(x, HEAD_SIZE // 2, 1)
+    return (x * cosine + turned * sine).astype(jnp.bfloat16)
+
+
+def lanes(piece, n):
+    return piece[:, n * HEAD_SIZE : (n + 1) * HEAD_SIZE]
+
+
+def stage_kernel(*refs):
+    slabs = (len(refs) - 6) // 2
+    own, other = refs[:slabs], refs[slabs : 2 * slabs]
+    cos_ref, sin_ref, k_ref, v_ref, ck_ref, cv_ref = refs[2 * slabs :]
     me = lax.axis_index("blk")
     chip, core = me // CORES, me % CORES
     rows = own[0].shape[0]
+    for j in range(slabs):
+        for piece, side in ((own[j], core), (other[j], 1 - core)):
+            at = pl.multiple_of(((chip ^ j) * CORES + side) * rows, rows)
+            here = pl.ds(at, rows)
+            k_ref[here] = rotate(lanes(piece, 0), cos_ref[here], sin_ref[here])
+            v_ref[here] = lanes(piece, 1)
+            ck_ref[here] = lanes(piece, 2)
+            cv_ref[here] = lanes(piece, 3)
+
+
+def attend_kernel(group, own_half, *refs):
+    queries, rest = refs[:-9], refs[-9:]
+    k_ref, v_ref, ck_ref, cv_ref, cos_ref, sin_ref, ctx_ref, out_ref, q_s = rest
+    slabs = len(queries)
+    me = lax.axis_index("blk")
+    chip, core = me // CORES, me % CORES
+    rows = queries[0].shape[0]
     span = rows * CORES
-
-    def lanes(piece, n):
-        return piece[:, n * HEAD_SIZE : (n + 1) * HEAD_SIZE]
-
-    def rotate(x, start):
-        x = x.astype(jnp.float32)
-        turned = pltpu.roll(x, HEAD_SIZE // 2, 1)
-        return (x * cos_ref[pl.ds(start, rows)] + turned * sin_ref[pl.ds(start, rows)]).astype(jnp.bfloat16)
-
-    for j in range(slabs):
+    half = lax.axis_index("heads") if own_half else 1 - lax.axis_index("heads")
+
+    def turn(j):
         source = chip ^ j
-        for piece, side in ((own[j], core), (other[j], 1 - core)):
-            at = pl.multiple_of(source * span + side * rows, rows)
-            k_s[pl.ds(at, rows)] = rotate(lanes(piece, 0), at)
-            v_s[pl.ds(at, rows)] = lanes(piece, 1)
-            ck_s[pl.ds(at, rows)] = lanes(piece, 2)
-            cv_s[pl.ds(at, rows)] = lanes(piece, 3)
-        start = pl.multiple_of(source * span + core * rows, rows)
+        here = pl.ds(pl.multiple_of(source * span + core * rows, rows), rows)
         for h in range(group):
             at = pl.multiple_of((source * group + h) * rows, rows)
-            q_s[pl.ds(at, rows)] = rotate(lanes(queries[j], h), start)
-
-    scale = 1.0 / math.sqrt(HEAD_SIZE)
+            q_s[pl.ds(at, rows)] = rotate(lanes(queries[j], h), cos_ref[here], sin_ref[here])
+
+    for j in range(slabs):
+        pl.when((chip ^ j) // (slabs // 2) == half)(functools.partial(turn, j))
+
+    scale = math.log2(math.e) / math.sqrt(HEAD_SIZE)
     height = group * rows
     total_rows = slabs * span
     cached_ok = lax.broadcasted_iota(jnp.int32, (1, total_rows), 1) < ctx_ref[0]
@@ -114,43 +131,35 @@
     row = lax.broadcasted_iota(jnp.int32, (height, span), 0) % rows + core * rows
     col = lax.broadcasted_iota(jnp.int32, (height, span), 1)
     diagonal = col <= row
-    contract_last = (((1,), (1,)), ((), ()))
+
+    def scores_of(q, keys):
+        dot = lax.dot_general(q, keys, (((1,), (1,)), ((), ())), preferred_element_type=jnp.float32)
+        return dot * scale
 
     def attend(blocks):
         for n, block in enumerate(blocks):
             q = q_s[block * height : (block + 1) * height]
-            cached = lax.dot_general(q, ck_s[...], contract_last, preferred_element_type=jnp.float32)
-            cached = cached * scale + cached_bias
-            top = jnp.max(cached, axis=1, keepdims=True)
-            parts = [(cached, cv_s[...])]
+            begin, end = block * span, (block + 1) * span
+            parts = [
+                (scores_of(q, ck_ref[...]) + cached_bias, cv_ref[...]),
+                (jnp.where(diagonal, scores_of(q, k_ref[begin:end]), NEG_FILL), v_ref[begin:end]),
+            ]
             if block:
-                past = lax.dot_general(
-                    q, k_s[: block * span], contract_last, preferred_element_type=jnp.float32
-                ) * scale
-                top = jnp.maximum(top, jnp.max(past, axis=1, keepdims=True))
-                parts.append((past, v_s[: block * span]))
-            near = lax.dot_general(
-                q, k_s[block * span : (block + 1) * span], contract_last, preferred_element_type=jnp.float32
-            ) * scale
-            near = jnp.where(diagonal, near, NEG_FILL)
-            top = jnp.maximum(top, jnp.max(near, axis=1, keepdims=True))
-            parts.append((near, v_s[block * span : (block + 1) * span]))
-            total = None
-            summed = None
+                parts.append((scores_of(q, k_ref[:begin]), v_ref[:begin]))
+            top = functools.reduce(jnp.maximum, [jnp.max(scores, axis=1, keepdims=True) for scores, _ in parts])
+            total, summed = 0.0, 0.0
             for scores, values in parts:
-                exp_scores = jnp.exp(scores - top)
-                part_total = jnp.sum(exp_scores, axis=1, keepdims=True)
-                part = jnp.dot(exp_scores.astype(jnp.bfloat16), values, preferred_element_type=jnp.float32)
-                total = part_total if total is None else total + part_total
-                summed = part if summed is None else summed + part
+                exp_scores = jnp.exp2(scores - top)
+                total = total + jnp.sum(exp_scores, axis=1, keepdims=True)
+                summed = summed + jnp.dot(
+                    exp_scores.astype(jnp.bfloat16), values, preferred_element_type=jnp.float32
+                )
             result = (summed / total).astype(jnp.bfloat16)
             for h in range(group):
                 out_ref[n, :, h * HEAD_SIZE : (h + 1) * HEAD_SIZE] = result[h * rows : (h + 1) * rows]
 
-    half = lax.axis_index("heads")
     for value in range(2):
-        which = value if own_half else 1 - value
-        blocks = tuple(range(which * slabs // 2, (which + 1) * slabs // 2))
+        blocks = tuple(range(value * slabs // 2, (value + 1) * slabs // 2))
         pl.when(half == value)(functools.partial(attend, blocks))
 
 
@@ -232,19 +241,28 @@
     swapped = [lax.ppermute(x, "blk", partner) for x in keys]
     half_chips = chips // 2
 
+    lined = jax.ShapeDtypeStruct((total_rows, HEAD_SIZE), jnp.bfloat16)
+    staged = pl.pallas_call(
+        stage_kernel,
+        out_shape=[lined] * 4,
+        in_specs=[whole()] * (2 * chips + 2),
+        out_specs=[whole()] * 4,
+        name="stage",
+        compiler_params=room(8),
+        cost_estimate=pl.CostEstimate(flops=1_000_000, bytes_accessed=1_000_000, transcendentals=0),
+    )(*keys, *swapped, cosine, sine)
+
     def attend(own_half):
         return pl.pallas_call(
             functools.partial(attend_kernel, group, own_half),
             out_shape=jax.ShapeDtypeStruct((half_chips, rows, width), jnp.bfloat16),
-            in_specs=[whole()] * (3 * chips + 2) + [whole(pltpu.SMEM)],
+            in_specs=[whole()] * (chips + 6) + [whole(pltpu.SMEM)],
             out_specs=whole(),
-            scratch_shapes=[pltpu.VMEM((chips * group * rows, HEAD_SIZE), jnp.bfloat16)]
-            + [pltpu.VMEM((total_rows, HEAD_SIZE), jnp.bfloat16)] * 4,
+            scratch_shapes=[pltpu.VMEM((chips * group * rows, HEAD_SIZE), jnp.bfloat16)],
             name="attend",
             compiler_params=room(12),
             cost_estimate=pl.CostEstimate(flops=400_000_000, bytes_accessed=1_000_000, transcendentals=600_000),
-        )(*queries, *keys, *swapped, cosine, sine, ctx_len)
-
+        )(*queries, *staged, cosine, sine, ctx_len)
 
     def project(distances, pieces, others, *added, dtype=jnp.bfloat16, final=False, column=0):
         count = pieces[0].shape[0] * CORES * rows
@@ -272,7 +290,9 @@
     far = lax.ppermute(sent, "blk", along(2))
     near = lax.ppermute(sent, "blk", along(1))
     pieces = [sent, near, far]
-    early = project((0, 1, 2), pieces, swap(pieces), dtype=jnp.float32)
+    others = swap(pieces)
+    early = project((0,), pieces[:1], others[:1], dtype=jnp.float32)
+    early = project((1, 2), pieces[1:], others[1:], early, dtype=jnp.float32)
     received = []
     for n in range(half_chips):
         relayed = lax.ppermute(far[n : n + 1], "blk", along(1))
@@ -282,7 +302,9 @@
     kept = attend(True)
     pieces = [kept] + [lax.ppermute(kept, "blk", along(j)) for j in (1, 2, 3)]
     others = swap(pieces)
-    return project((0, 1, 2, 3), pieces, others, jnp.concatenate(received, axis=1), final=True)
+    early = project((0,), pieces[:1], others[:1], dtype=jnp.float32)
+    received = jnp.concatenate(received, axis=1)
+    return project((1, 2, 3), pieces[1:], others[1:], early, received, final=True)
 
 
 def rotary(inputs, positions):

time: 60.8 us -> 60.4 us (level)
  waiting for transfers between devices: 25.4 us -> 23.2 us
  starting transfers between devices: 22.8 us -> 23.8 us
    ppermute x1, waiting for transfers between devices: 2.02 us -> 6.28 us  [head_sharded(): far = lax.ppermute(sent, 'blk', along(2))]
    ppermute x1, waiting for transfers between devices: 5.77 us -> 1.81 us  [head_sharded(): near = lax.ppermute(sent, 'blk', along(1))]
    ppermute x2, waiting for transfers between devices: 3.29 us -> 1.62 us  [head_sharded(): relayed = lax.ppermute(far[n:n + 1], 'blk', along(1))]
    ppermute x2, starting transfers between devices: 2.09 us -> 1.01 us  [head_sharded(): relayed = lax.ppermute(far[n:n + 1], 'blk', along(1))]
    ppermute x7, waiting for transfers between devices: 1.28 us -> 0.56 us  [swap(): return [lax.ppermute(piece, 'blk', partner) for piece in pieces]]
    ppermute x3, waiting for transfers between devices: 8.36 us -> 7.72 us  [head_sharded(): pieces = [kept] + [lax.ppermute(kept, 'blk', along(j)) for j in (1, 2, 3)]]
    pallas_call x4 -> x6, Pallas kernels: 3.73 us -> 4.27 us  [project(): pl.pallas_call(functools.partial(project_kernel, distances, final, column...]
  transfers between devices with their start and end apart: 28 -> 28, of which waited for: 10 -> 10; matrix products, arithmetic and copies ran while one was open for 2% -> 2% of each run, Pallas kernels for 8% -> 9%
where the time goes in v2:
time: 60.4 us; the launch traced here: 59.8 us
  starting transfers between devices  23.8 us (39%)
  waiting for transfers between devices  23.2 us (38%)
  Pallas kernels  9.96 us (16%)
  between operations  1.56 us (3%)
  other arithmetic  1.25 us (2%)
    ppermute x3, waiting for transfers between devices, head_sharded(): pieces = [kept] + [lax.ppermute(kept, 'blk', along(j)) for j in (1, 2, 3)]  7.72 us
    ppermute x1, waiting for transfers between devices, head_sharded(): far = lax.ppermute(sent, 'blk', along(2))  6.28 us
    ppermute x3, starting transfers between devices, head_sharded(): lax.ppermute(keyed[j], 'blk', along(j))  5.71 us
    ppermute x3, waiting for transfers between devices, head_sharded(): lax.ppermute(asked[j], 'blk', along(j))  4.96 us
    ppermute x3, starting transfers between devices, head_sharded(): lax.ppermute(asked[j], 'blk', along(j))  4.45 us
    ppermute x3, starting transfers between devices, head_sharded(): pieces = [kept] + [lax.ppermute(kept, 'blk', along(j)) for j in (1, 2, 3)]  4.45 us
    pallas_call x6, Pallas kernels, project(): pl.pallas_call(functools.partial(project_kernel, distances, final, column...  4.27 us
    pallas_call x2, Pallas kernels, attend(): pl.pallas_call(functools.partial(attend_kernel, group, own_half), out_sha...  2.91 us
  transfers between devices with their start and end apart: 28, of which 10 were waited for; matrix products, arithmetic and copies ran while one was open for 2% of the time, Pallas kernels for 9%

profile of v2, /device:TPU:0, one launch (start us, length us, event | category | flops | bytes accessed | tf_op | source)
XLA Modules:
  0.0 59.8 jit_solution(12649342916926263905)
XLA Ops:
  0.0 1.3 %shard_map.83 = (bf16[64,512]{1,0:T(8,128)(2,1)S(1)}, bf16[64,512]{1,0:T(8,128)(2,1)S(1)}, bf16[64,512]{1,0:T(8,128)(2,1)S(1)}, bf16[64,512]{1,0:T(8,128)(2,1)S(1)}) custom-call(bf16[64,512]{1,0:T(8,128)(2,1)} %refs_0_.3, bf16[64,512]{1,0:T(8,128)(2,1)} %refs_1_.1, bf16[64,512]{1,0:T(8,128)(2,1)} %refs_2_.1, bf16[64,512]{1,0:T(8,128)(2,1)} %refs_3_.1), custom_call_target="tpu_custom_call" | custom-call | tf_op jit(solution)/shard_map/pallas_call | solution.py:66
  1.3 3.1 %collective-permute-start.3 = (bf16[64,512]{1,0:T(8,128)(2,1)S(1)}, bf16[64,512]{1,0:T(8,128)(2,1)S(1)}, u32[]{:S(2)}, u32[]{:S(2)}) collective-permute-start(bf16[64,512]{1,0:T(8,128)(2,1)S(1)} %get-tuple-element.28), channel_id=1, source_target_pairs={{0,4},{2,6},{4,0},{6,2},{8,12},{10,14},{12,8},{14,10},{1,5},{3,7},... | collective-permute-start | bytes 196616 | tf_op jit(solution)/shard_map/ppermute | solution.py:237
  4.4 2.6 %collective-permute-start.4 = (bf16[64,512]{1,0:T(8,128)(2,1)S(1)}, bf16[64,512]{1,0:T(8,128)(2,1)S(1)}, u32[]{:S(2)}, u32[]{:S(2)}) collective-permute-start(bf16[64,512]{1,0:T(8,128)(2,1)S(1)} %get-tuple-element.33), channel_id=1, source_target_pairs={{0,8},{2,10},{4,12},{6,14},{8,0},{10,2},{12,4},{14,6},{1,9},{3,11}... | collective-permute-start | bytes 196616 | tf_op jit(solution)/shard_map/ppermute | solution.py:237
  7.0 0.0 collective-permute-start.5
  7.7 0.0 copy-start
  7.7 1.0 %fusion = (f32[512,64]{1,0:T(8,128)S(1)}, f32[512,64]{1,0:T(8,128)S(1)}, f32[512,64]{1,0:T(8,128)S(1)}) fusion(f32[64]{0:T(128)S(1)} %negate_power_fusion, f32[512]{0:T(512)S(1)} %add_convert_fusion), kind=kLoop, calls=%fused_computation.5 | loop fusion | flops 65536 | bytes 395520 | tf_op jit(solution)/shard_map/neg | solution.py:235
  8.7 0.2 pad_maximum_fusion.1
  8.9 0.0 collective-permute-done.3.refs_1_
  8.9 0.1 collective-permute-start.6
  9.0 0.5 collective-permute-start.7
  9.5 1.3 %shard_map.82 = (bf16[64,640]{1,0:T(8,128)(2,1)S(1)}, bf16[64,640]{1,0:T(8,128)(2,1)S(1)}, bf16[64,640]{1,0:T(8,128)(2,1)S(1)}, bf16[64,640]{1,0:T(8,128)(2,1)S(1)}) custom-call(bf16[64,2560]{1,0:T(8,128)(2,1)} %refs_0_.2), custom_call_target="tpu_custom_call" | custom-call | tf_op jit(solution)/shard_map/pallas_call | solution.py:66
  10.9 1.0 %collective-permute-start = (bf16[64,640]{1,0:T(8,128)(2,1)S(1)}, bf16[64,640]{1,0:T(8,128)(2,1)S(1)}, u32[]{:S(2)}, u32[]{:S(2)}) collective-permute-start(bf16[64,640]{1,0:T(8,128)(2,1)S(1)} %get-tuple-element.24), channel_id=1, source_target_pairs={{0,4},{2,6},{4,0},{6,2},{8,12},{10,14},{12,8},{14,10},{1,5},{3,7},... | collective-permute-start | bytes 245768 | tf_op jit(solution)/shard_map/ppermute | solution.py:238
  11.8 3.5 %collective-permute-start.1 = (bf16[64,640]{1,0:T(8,128)(2,1)S(1)}, bf16[64,640]{1,0:T(8,128)(2,1)S(1)}, u32[]{:S(2)}, u32[]{:S(2)}) collective-permute-start(bf16[64,640]{1,0:T(8,128)(2,1)S(1)} %get-tuple-element.25), channel_id=1, source_target_pairs={{0,8},{2,10},{4,12},{6,14},{8,0},{10,2},{12,4},{14,6},{1,9},{3,11}... | collective-permute-start | bytes 245768 | tf_op jit(solution)/shard_map/ppermute | solution.py:238
  15.3 0.0 collective-permute-start.2
  15.3 0.1 collective-permute-start.8
  15.4 0.5 collective-permute-start.9
  16.6 0.1 collective-permute-done.8.refs_6_
  16.6 0.2 collective-permute-done.9.refs_7_
  16.8 0.1 stage.1
  17.0 5.0 %collective-permute-done.1.refs_2_ = bf16[64,640]{1,0:T(8,128)(2,1)S(1)} collective-permute-done((bf16[64,640]{1,0:T(8,128)(2,1)S(1)}, bf16[64,640]{1,0:T(8,128)(2,1)S(1)}, u32[]{:S(2)}, u32[]{:S(2)}) %collective-permute-start.1) | collective-permute-done | bytes 81952 | tf_op jit(solution)/shard_map/ppermute | solution.py:238
  21.9 1.5 %attend.3.refs_0_ = bf16[2,64,640]{2,1,0:T(8,128)(2,1)S(1)} custom-call(bf16[64,640]{1,0:T(8,128)(2,1)S(1)} %get-tuple-element.23.refs_0_, bf16[64,640]{1,0:T(8,128)(2,1)S(1)} %collective-permute-done.refs_1_, bf16[64,640]{1,0:T(8,128)(2,1)S(1)} %collective-permute-done.1.refs_2_, bf16[64,640]{1,0:T(8,128)(2,1)S(1)} %collective-permute-done.2.refs_3_, ...), custom_call_target="tpu_custom_call" | custom-call | flops 400000000 | bytes 1000000 | tf_op jit(solution)/shard_map/attend/pallas_call | solution.py:256
  23.5 2.7 %collective-permute-start.17 = (bf16[2,64,640]{2,1,0:T(8,128)(2,1)S(1)}, bf16[2,64,640]{2,1,0:T(8,128)(2,1)S(1)}, u32[]{:S(2)}, u32[]{:S(2)}) collective-permute-start(bf16[2,64,640]{2,1,0:T(8,128)(2,1)S(1)} %attend.3.refs_0_), channel_id=1, source_target_pairs={{0,8},{2,10},{4,12},{6,14},{8,0},{10,2},{12,4},{14,6},{1,9},{3,11}... | collective-permute-start | bytes 491528 | tf_op jit(solution)/shard_map/ppermute | solution.py:290
  26.2 0.6 collective-permute-start.20
  26.7 6.3 %collective-permute-done.17.refs_1_ = bf16[2,64,640]{2,1,0:T(8,128)(2,1)S(1)} collective-permute-done((bf16[2,64,640]{2,1,0:T(8,128)(2,1)S(1)}, bf16[2,64,640]{2,1,0:T(8,128)(2,1)S(1)}, u32[]{:S(2)}, u32[]{:S(2)}) %collective-permute-start.17) | collective-permute-done | bytes 163872 | tf_op jit(solution)/shard_map/ppermute | solution.py:290
  33.0 0.2 collective-permute-start.18
  33.2 1.8 %collective-permute-done.20.refs_0_ = bf16[2,64,640]{2,1,0:T(8,128)(2,1)S(1)} collective-permute-done((bf16[2,64,640]{2,1,0:T(8,128)(2,1)S(1)}, bf16[2,64,640]{2,1,0:T(8,128)(2,1)S(1)}, u32[]{:S(2)}, u32[]{:S(2)}) %collective-permute-start.20) | collective-permute-done | bytes 163872 | tf_op jit(solution)/shard_map/ppermute | solution.py:291
  35.0 0.5 collective-permute-start.22
  35.5 0.8 %collective-permute-start.25 = (bf16[1,64,640]{2,1,0:T(8,128)(2,1)S(1)}, bf16[1,64,640]{2,1,0:T(8,128)(2,1)S(1)}, u32[]{:S(2)}, u32[]{:S(2)}) collective-permute-start(bf16[1,64,640]{2,1,0:T(8,128)(2,1)S(1)} %get-tuple-element.42), channel_id=1, source_target_pairs={{0,4},{2,6},{4,0},{6,2},{8,12},{10,14},{12,8},{14,10},{1,5},{3,7},... | collective-permute-start | bytes 245768 | tf_op jit(solution)/shard_map/ppermute | solution.py:298
  36.4 1.4 %attend.2.refs_0_ = bf16[2,64,640]{2,1,0:T(8,128)(2,1)S(1)} custom-call(bf16[64,640]{1,0:T(8,128)(2,1)S(1)} %get-tuple-element.23.refs_0_, bf16[64,640]{1,0:T(8,128)(2,1)S(1)} %collective-permute-done.refs_1_, bf16[64,640]{1,0:T(8,128)(2,1)S(1)} %collective-permute-done.1.refs_2_, bf16[64,640]{1,0:T(8,128)(2,1)S(1)} %collective-permute-done.2.refs_3_, ...), custom_call_target="tpu_custom_call" | custom-call | flops 400000000 | bytes 1000000 | tf_op jit(solution)/shard_map/attend/pallas_call | solution.py:256
  37.8 0.1 collective-permute-start.16
  37.9 0.5 collective-permute-start.19
  38.3 1.6 %collective-permute-done.25.refs_0_ = bf16[1,64,640]{2,1,0:T(8,128)(2,1)S(1)} collective-permute-done((bf16[1,64,640]{2,1,0:T(8,128)(2,1)S(1)}, bf16[1,64,640]{2,1,0:T(8,128)(2,1)S(1)}, u32[]{:S(2)}, u32[]{:S(2)}) %collective-permute-start.25) | collective-permute-done | bytes 81952 | tf_op jit(solution)/shard_map/ppermute | solution.py:298
  40.0 0.5 project.7.refs_4_
  40.5 0.9 %collective-permute-start.10 = (bf16[2,64,640]{2,1,0:T(8,128)(2,1)S(1)}, bf16[2,64,640]{2,1,0:T(8,128)(2,1)S(1)}, u32[]{:S(2)}, u32[]{:S(2)}) collective-permute-start(bf16[2,64,640]{2,1,0:T(8,128)(2,1)S(1)} %attend.2.refs_0_), channel_id=1, source_target_pairs={{0,4},{2,6},{4,0},{6,2},{8,12},{10,14},{12,8},{14,10},{1,5},{3,7},... | collective-permute-start | bytes 491528 | tf_op jit(solution)/shard_map/ppermute | solution.py:303
  41.4 1.1 %collective-permute-start.11 = (bf16[2,64,640]{2,1,0:T(8,128)(2,1)S(1)}, bf16[2,64,640]{2,1,0:T(8,128)(2,1)S(1)}, u32[]{:S(2)}, u32[]{:S(2)}) collective-permute-start(bf16[2,64,640]{2,1,0:T(8,128)(2,1)S(1)} %attend.2.refs_0_), channel_id=1, source_target_pairs={{0,8},{2,10},{4,12},{6,14},{8,0},{10,2},{12,4},{14,6},{1,9},{3,11}... | collective-permute-start | bytes 491528 | tf_op jit(solution)/shard_map/ppermute | solution.py:303
  42.4 2.5 %collective-permute-start.12 = (bf16[2,64,640]{2,1,0:T(8,128)(2,1)S(1)}, bf16[2,64,640]{2,1,0:T(8,128)(2,1)S(1)}, u32[]{:S(2)}, u32[]{:S(2)}) collective-permute-start(bf16[2,64,640]{2,1,0:T(8,128)(2,1)S(1)} %attend.2.refs_0_), channel_id=1, source_target_pairs={{0,12},{2,14},{4,8},{6,10},{8,4},{10,6},{12,0},{14,2},{1,13},{3,15... | collective-permute-start | bytes 491528 | tf_op jit(solution)/shard_map/ppermute | solution.py:303
  44.9 0.8 %project.8.refs_2_ = f32[640,256]{1,0:T(8,128)S(1)} custom-call(bf16[640,2560]{1,0:T(8,128)(2,1)S(1)} %copy-done, bf16[2,64,640]{2,1,0:T(8,128)(2,1)S(1)} %collective-permute-done.20.refs_0_, bf16[2,64,640]{2,1,0:T(8,128)(2,1)S(1)} %collective-permute-done.17.refs_1_, bf16[2,64,640]{2,1,0:T(8,128)(2,1)S(1)} %collective-permute-done.21.refs_2_, ...), custom_call_target="tpu_custom_call" | custom-call | flops 419430400 | bytes 1000000 | tf_op jit(solution)/shard_map/project/pallas_call | solution.py:273
  45.7 0.4 project.9
  46.1 1.3 %collective-permute-start.24 = (bf16[640,128]{1,0:T(8,128)(2,1)S(1)}, bf16[640,128]{1,0:T(8,128)(2,1)S(1)}, u32[]{:S(2)}, u32[]{:S(2)}) collective-permute-start(bf16[640,128]{1,0:T(8,128)(2,1)S(1)} %project.9), channel_id=1, source_target_pairs={{0,1},{1,0},{2,3},{3,2},{4,5},{5,4},{6,7},{7,6},{8,9},{9,8},{10,11... | collective-permute-start | bytes 491528 | tf_op jit(solution)/shard_map/ppermute | solution.py:301
  47.5 0.4 project.10
  47.9 0.8 %collective-permute-start.27 = (bf16[640,128]{1,0:T(8,128)(2,1)S(1)}, bf16[640,128]{1,0:T(8,128)(2,1)S(1)}, u32[]{:S(2)}, u32[]{:S(2)}) collective-permute-start(bf16[640,128]{1,0:T(8,128)(2,1)S(1)} %project.10), channel_id=1, source_target_pairs={{0,1},{1,0},{2,3},{3,2},{4,5},{5,4},{6,7},{7,6},{8,9},{9,8},{10,11... | collective-permute-start | bytes 491528 | tf_op jit(solution)/shard_map/ppermute | solution.py:301
  48.7 1.0 %collective-permute-done.10.refs_0_ = bf16[2,64,640]{2,1,0:T(8,128)(2,1)S(1)} collective-permute-done((bf16[2,64,640]{2,1,0:T(8,128)(2,1)S(1)}, bf16[2,64,640]{2,1,0:T(8,128)(2,1)S(1)}, u32[]{:S(2)}, u32[]{:S(2)}) %collective-permute-start.10) | collective-permute-done | bytes 163872 | tf_op jit(solution)/shard_map/ppermute | solution.py:303
  49.7 6.7 %collective-permute-done.11.refs_1_ = bf16[2,64,640]{2,1,0:T(8,128)(2,1)S(1)} collective-permute-done((bf16[2,64,640]{2,1,0:T(8,128)(2,1)S(1)}, bf16[2,64,640]{2,1,0:T(8,128)(2,1)S(1)}, u32[]{:S(2)}, u32[]{:S(2)}) %collective-permute-start.11) | collective-permute-done | bytes 163872 | tf_op jit(solution)/shard_map/ppermute | solution.py:303
  56.4 0.5 collective-permute-start.15
  56.9 0.5 project.6.refs_6_
  57.5 0.3 collective-permute-done.14.refs_4_
  57.8 0.2 collective-permute-done.15.refs_5_
  58.1 1.7 %project.11 = bf16[640,256]{1,0:T(8,128)(2,1)} custom-call(bf16[640,2560]{1,0:T(8,128)(2,1)S(1)} %copy-done, bf16[2,64,640]{2,1,0:T(8,128)(2,1)S(1)} %collective-permute-done.10.refs_0_, bf16[2,64,640]{2,1,0:T(8,128)(2,1)S(1)} %collective-permute-done.11.refs_1_, bf16[2,64,640]{2,1,0:T(8,128)(2,1)S(1)} %collective-permute-done.12.refs_2_, ...), custom_call_target="tpu_custom_call" | custom-call | flops 629145600 | bytes 1000000 | tf_op jit(solution)/shard_map/project/pallas_call | solution.py:273
  (27 shorter events, 0.1 us)
Async XLA Ops:
  1.3 7.6 %collective-permute-start.3 = (bf16[64,512]{1,0:T(8,128)(2,1)S(1)}, bf16[64,512]{1,0:T(8,128)(2,1)S(1)}, u32[]{:S(2)}, u32[]{:S(2)}) collective-permute-start(bf16[64,512]{1,0:T(8,128)(2,1)S(1)} %get-tuple-element.28), channel_id=1, source_target_pairs={{0,4},{2,6},{4,0},{6,2},{8,12},{10,14},{12,8},{14,10},{1,5},{3,7},... | collective-permute-start | bytes 196616 | tf_op jit(solution)/shard_map/ppermute | solution.py:237
  4.4 7.4 %collective-permute-start.4 = (bf16[64,512]{1,0:T(8,128)(2,1)S(1)}, bf16[64,512]{1,0:T(8,128)(2,1)S(1)}, u32[]{:S(2)}, u32[]{:S(2)}) collective-permute-start(bf16[64,512]{1,0:T(8,128)(2,1)S(1)} %get-tuple-element.33), channel_id=1, source_target_pairs={{0,8},{2,10},{4,12},{6,14},{8,0},{10,2},{12,4},{14,6},{1,9},{3,11}... | collective-permute-start | bytes 196616 | tf_op jit(solution)/shard_map/ppermute | solution.py:237
  7.0 8.3 %collective-permute-start.5 = (bf16[64,512]{1,0:T(8,128)(2,1)S(1)}, bf16[64,512]{1,0:T(8,128)(2,1)S(1)}, u32[]{:S(2)}, u32[]{:S(2)}) collective-permute-start(bf16[64,512]{1,0:T(8,128)(2,1)S(1)} %get-tuple-element.34), channel_id=1, source_target_pairs={{0,12},{2,14},{4,8},{6,10},{8,4},{10,6},{12,0},{14,2},{1,13},{3,15... | collective-permute-start | bytes 196616 | tf_op jit(solution)/shard_map/ppermute | solution.py:237
  7.7 32.3 %copy-start = (bf16[640,2560]{1,0:T(8,128)(2,1)S(1)}, bf16[640,2560]{1,0:T(8,128)(2,1)}, u32[]{:S(2)}) copy-start(bf16[640,2560]{1,0:T(8,128)(2,1)} %w_ref.11) | copy-start | bytes 9830404
  8.9 6.4 %collective-permute-start.6 = (bf16[64,512]{1,0:T(8,128)(2,1)S(1)}, bf16[64,512]{1,0:T(8,128)(2,1)S(1)}, u32[]{:S(2)}, u32[]{:S(2)}) collective-permute-start(bf16[64,512]{1,0:T(8,128)(2,1)S(1)} %get-tuple-element.31.refs_0_), channel_id=1, source_target_pairs={{0,2},{2,0},{4,6},{6,4},{8,10},{10,8},{12,14},{14,12},{1,3},{3,1},... | collective-permute-start | bytes 196616 | tf_op jit(solution)/shard_map/ppermute | solution.py:241
  9.0 6.4 %collective-permute-start.7 = (bf16[64,512]{1,0:T(8,128)(2,1)S(1)}, bf16[64,512]{1,0:T(8,128)(2,1)S(1)}, u32[]{:S(2)}, u32[]{:S(2)}) collective-permute-start(bf16[64,512]{1,0:T(8,128)(2,1)S(1)} %collective-permute-done.3.refs_1_), channel_id=1, source_target_pairs={{0,2},{2,0},{4,6},{6,4},{8,10},{10,8},{12,14},{14,12},{1,3},{3,1},... | collective-permute-start | bytes 196616 | tf_op jit(solution)/shard_map/ppermute | solution.py:241
  10.9 6.1 %collective-permute-start = (bf16[64,640]{1,0:T(8,128)(2,1)S(1)}, bf16[64,640]{1,0:T(8,128)(2,1)S(1)}, u32[]{:S(2)}, u32[]{:S(2)}) collective-permute-start(bf16[64,640]{1,0:T(8,128)(2,1)S(1)} %get-tuple-element.24), channel_id=1, source_target_pairs={{0,4},{2,6},{4,0},{6,2},{8,12},{10,14},{12,8},{14,10},{1,5},{3,7},... | collective-permute-start | bytes 245768 | tf_op jit(solution)/shard_map/ppermute | solution.py:238
  11.8 10.1 %collective-permute-start.1 = (bf16[64,640]{1,0:T(8,128)(2,1)S(1)}, bf16[64,640]{1,0:T(8,128)(2,1)S(1)}, u32[]{:S(2)}, u32[]{:S(2)}) collective-permute-start(bf16[64,640]{1,0:T(8,128)(2,1)S(1)} %get-tuple-element.25), channel_id=1, source_target_pairs={{0,8},{2,10},{4,12},{6,14},{8,0},{10,2},{12,4},{14,6},{1,9},{3,11}... | collective-permute-start | bytes 245768 | tf_op jit(solution)/shard_map/ppermute | solution.py:238
  15.3 6.6 %collective-permute-start.2 = (bf16[64,640]{1,0:T(8,128)(2,1)S(1)}, bf16[64,640]{1,0:T(8,128)(2,1)S(1)}, u32[]{:S(2)}, u32[]{:S(2)}) collective-permute-start(bf16[64,640]{1,0:T(8,128)(2,1)S(1)} %get-tuple-element.26), channel_id=1, source_target_pairs={{0,12},{2,14},{4,8},{6,10},{8,4},{10,6},{12,0},{14,2},{1,13},{3,15... | collective-permute-start | bytes 245768 | tf_op jit(solution)/shard_map/ppermute | solution.py:238
  15.3 1.3 %collective-permute-start.8 = (bf16[64,512]{1,0:T(8,128)(2,1)S(1)}, bf16[64,512]{1,0:T(8,128)(2,1)S(1)}, u32[]{:S(2)}, u32[]{:S(2)}) collective-permute-start(bf16[64,512]{1,0:T(8,128)(2,1)S(1)} %collective-permute-done.4.refs_2_), channel_id=1, source_target_pairs={{0,2},{2,0},{4,6},{6,4},{8,10},{10,8},{12,14},{14,12},{1,3},{3,1},... | collective-permute-start | bytes 196616 | tf_op jit(solution)/shard_map/ppermute | solution.py:241
  15.4 1.4 %collective-permute-start.9 = (bf16[64,512]{1,0:T(8,128)(2,1)S(1)}, bf16[64,512]{1,0:T(8,128)(2,1)S(1)}, u32[]{:S(2)}, u32[]{:S(2)}) collective-permute-start(bf16[64,512]{1,0:T(8,128)(2,1)S(1)} %collective-permute-done.5.refs_3_), channel_id=1, source_target_pairs={{0,2},{2,0},{4,6},{6,4},{8,10},{10,8},{12,14},{14,12},{1,3},{3,1},... | collective-permute-start | bytes 196616 | tf_op jit(solution)/shard_map/ppermute | solution.py:241
  23.5 9.6 %collective-permute-start.17 = (bf16[2,64,640]{2,1,0:T(8,128)(2,1)S(1)}, bf16[2,64,640]{2,1,0:T(8,128)(2,1)S(1)}, u32[]{:S(2)}, u32[]{:S(2)}) collective-permute-start(bf16[2,64,640]{2,1,0:T(8,128)(2,1)S(1)} %attend.3.refs_0_), channel_id=1, source_target_pairs={{0,8},{2,10},{4,12},{6,14},{8,0},{10,2},{12,4},{14,6},{1,9},{3,11}... | collective-permute-start | bytes 491528 | tf_op jit(solution)/shard_map/ppermute | solution.py:290
  26.2 11.6 %collective-permute-start.23 = (bf16[2,64,640]{2,1,0:T(8,128)(2,1)S(1)}, bf16[2,64,640]{2,1,0:T(8,128)(2,1)S(1)}, u32[]{:S(2)}, u32[]{:S(2)}) collective-permute-start(bf16[2,64,640]{2,1,0:T(8,128)(2,1)S(1)} %attend.3.refs_0_), channel_id=1, source_target_pairs={{0,2},{2,0},{4,6},{6,4},{8,10},{10,8},{12,14},{14,12},{1,3},{3,1},... | collective-permute-start | bytes 491528 | tf_op jit(solution)/shard_map/ppermute | solution.py:287
  26.2 8.9 %collective-permute-start.20 = (bf16[2,64,640]{2,1,0:T(8,128)(2,1)S(1)}, bf16[2,64,640]{2,1,0:T(8,128)(2,1)S(1)}, u32[]{:S(2)}, u32[]{:S(2)}) collective-permute-start(bf16[2,64,640]{2,1,0:T(8,128)(2,1)S(1)} %attend.3.refs_0_), channel_id=1, source_target_pairs={{0,4},{2,6},{4,0},{6,2},{8,12},{10,14},{12,8},{14,10},{1,5},{3,7},... | collective-permute-start | bytes 491528 | tf_op jit(solution)/shard_map/ppermute | solution.py:291
  33.0 4.8 %collective-permute-start.18 = (bf16[1,64,640]{2,1,0:T(8,128)(2,1)S(1)}, bf16[1,64,640]{2,1,0:T(8,128)(2,1)S(1)}, u32[]{:S(2)}, u32[]{:S(2)}) collective-permute-start(bf16[1,64,640]{2,1,0:T(8,128)(2,1)S(1)} %get-tuple-element.41), channel_id=1, source_target_pairs={{0,4},{2,6},{4,0},{6,2},{8,12},{10,14},{12,8},{14,10},{1,5},{3,7},... | collective-permute-start | bytes 245768 | tf_op jit(solution)/shard_map/ppermute | solution.py:298
  35.0 6.4 %collective-permute-start.21 = (bf16[2,64,640]{2,1,0:T(8,128)(2,1)S(1)}, bf16[2,64,640]{2,1,0:T(8,128)(2,1)S(1)}, u32[]{:S(2)}, u32[]{:S(2)}) collective-permute-start(bf16[2,64,640]{2,1,0:T(8,128)(2,1)S(1)} %collective-permute-done.20.refs_0_), channel_id=1, source_target_pairs={{0,2},{2,0},{4,6},{6,4},{8,10},{10,8},{12,14},{14,12},{1,3},{3,1},... | collective-permute-start | bytes 491528 | tf_op jit(solution)/shard_map/ppermute | solution.py:287
  35.0 7.4 %collective-permute-start.22 = (bf16[2,64,640]{2,1,0:T(8,128)(2,1)S(1)}, bf16[2,64,640]{2,1,0:T(8,128)(2,1)S(1)}, u32[]{:S(2)}, u32[]{:S(2)}) collective-permute-start(bf16[2,64,640]{2,1,0:T(8,128)(2,1)S(1)} %collective-permute-done.17.refs_1_), channel_id=1, source_target_pairs={{0,2},{2,0},{4,6},{6,4},{8,10},{10,8},{12,14},{14,12},{1,3},{3,1},... | collective-permute-start | bytes 491528 | tf_op jit(solution)/shard_map/ppermute | solution.py:287
  35.5 4.4 %collective-permute-start.25 = (bf16[1,64,640]{2,1,0:T(8,128)(2,1)S(1)}, bf16[1,64,640]{2,1,0:T(8,128)(2,1)S(1)}, u32[]{:S(2)}, u32[]{:S(2)}) collective-permute-start(bf16[1,64,640]{2,1,0:T(8,128)(2,1)S(1)} %get-tuple-element.42), channel_id=1, source_target_pairs={{0,4},{2,6},{4,0},{6,2},{8,12},{10,14},{12,8},{14,10},{1,5},{3,7},... | collective-permute-start | bytes 245768 | tf_op jit(solution)/shard_map/ppermute | solution.py:298
  37.8 10.1 %collective-permute-start.16 = (bf16[2,64,640]{2,1,0:T(8,128)(2,1)S(1)}, bf16[2,64,640]{2,1,0:T(8,128)(2,1)S(1)}, u32[]{:S(2)}, u32[]{:S(2)}) collective-permute-start(bf16[2,64,640]{2,1,0:T(8,128)(2,1)S(1)} %attend.2.refs_0_), channel_id=1, source_target_pairs={{0,2},{2,0},{4,6},{6,4},{8,10},{10,8},{12,14},{14,12},{1,3},{3,1},... | collective-permute-start | bytes 491528 | tf_op jit(solution)/shard_map/ppermute | solution.py:287
  37.9 2.6 %collective-permute-start.19 = (bf16[1,64,640]{2,1,0:T(8,128)(2,1)S(1)}, bf16[1,64,640]{2,1,0:T(8,128)(2,1)S(1)}, u32[]{:S(2)}, u32[]{:S(2)}) collective-permute-start(bf16[1,64,640]{2,1,0:T(8,128)(2,1)S(1)} %collective-permute-done.18.refs_0_), channel_id=1, source_target_pairs={{0,2},{2,0},{4,6},{6,4},{8,10},{10,8},{12,14},{14,12},{1,3},{3,1},... | collective-permute-start | bytes 245768 | tf_op jit(solution)/shard_map/ppermute | solution.py:299
  40.0 6.2 %collective-permute-start.26 = (bf16[1,64,640]{2,1,0:T(8,128)(2,1)S(1)}, bf16[1,64,640]{2,1,0:T(8,128)(2,1)S(1)}, u32[]{:S(2)}, u32[]{:S(2)}) collective-permute-start(bf16[1,64,640]{2,1,0:T(8,128)(2,1)S(1)} %collective-permute-done.25.refs_0_), channel_id=1, source_target_pairs={{0,2},{2,0},{4,6},{6,4},{8,10},{10,8},{12,14},{14,12},{1,3},{3,1},... | collective-permute-start | bytes 245768 | tf_op jit(solution)/shard_map/ppermute | solution.py:299
  40.5 9.2 %collective-permute-start.10 = (bf16[2,64,640]{2,1,0:T(8,128)(2,1)S(1)}, bf16[2,64,640]{2,1,0:T(8,128)(2,1)S(1)}, u32[]{:S(2)}, u32[]{:S(2)}) collective-permute-start(bf16[2,64,640]{2,1,0:T(8,128)(2,1)S(1)} %attend.2.refs_0_), channel_id=1, source_target_pairs={{0,4},{2,6},{4,0},{6,2},{8,12},{10,14},{12,8},{14,10},{1,5},{3,7},... | collective-permute-start | bytes 491528 | tf_op jit(solution)/shard_map/ppermute | solution.py:303
  41.4 15.0 %collective-permute-start.11 = (bf16[2,64,640]{2,1,0:T(8,128)(2,1)S(1)}, bf16[2,64,640]{2,1,0:T(8,128)(2,1)S(1)}, u32[]{:S(2)}, u32[]{:S(2)}) collective-permute-start(bf16[2,64,640]{2,1,0:T(8,128)(2,1)S(1)} %attend.2.refs_0_), channel_id=1, source_target_pairs={{0,8},{2,10},{4,12},{6,14},{8,0},{10,2},{12,4},{14,6},{1,9},{3,11}... | collective-permute-start | bytes 491528 | tf_op jit(solution)/shard_map/ppermute | solution.py:303
  42.4 14.0 %collective-permute-start.12 = (bf16[2,64,640]{2,1,0:T(8,128)(2,1)S(1)}, bf16[2,64,640]{2,1,0:T(8,128)(2,1)S(1)}, u32[]{:S(2)}, u32[]{:S(2)}) collective-permute-start(bf16[2,64,640]{2,1,0:T(8,128)(2,1)S(1)} %attend.2.refs_0_), channel_id=1, source_target_pairs={{0,12},{2,14},{4,8},{6,10},{8,4},{10,6},{12,0},{14,2},{1,13},{3,15... | collective-permute-start | bytes 491528 | tf_op jit(solution)/shard_map/ppermute | solution.py:303
  46.1 11.3 %collective-permute-start.24 = (bf16[640,128]{1,0:T(8,128)(2,1)S(1)}, bf16[640,128]{1,0:T(8,128)(2,1)S(1)}, u32[]{:S(2)}, u32[]{:S(2)}) collective-permute-start(bf16[640,128]{1,0:T(8,128)(2,1)S(1)} %project.9), channel_id=1, source_target_pairs={{0,1},{1,0},{2,3},{3,2},{4,5},{5,4},{6,7},{7,6},{8,9},{9,8},{10,11... | collective-permute-start | bytes 491528 | tf_op jit(solution)/shard_map/ppermute | solution.py:301
  47.9 9.6 %collective-permute-start.27 = (bf16[640,128]{1,0:T(8,128)(2,1)S(1)}, bf16[640,128]{1,0:T(8,128)(2,1)S(1)}, u32[]{:S(2)}, u32[]{:S(2)}) collective-permute-start(bf16[640,128]{1,0:T(8,128)(2,1)S(1)} %project.10), channel_id=1, source_target_pairs={{0,1},{1,0},{2,3},{3,2},{4,5},{5,4},{6,7},{7,6},{8,9},{9,8},{10,11... | collective-permute-start | bytes 491528 | tf_op jit(solution)/shard_map/ppermute | solution.py:301
  49.7 7.8 %collective-permute-start.13 = (bf16[2,64,640]{2,1,0:T(8,128)(2,1)S(1)}, bf16[2,64,640]{2,1,0:T(8,128)(2,1)S(1)}, u32[]{:S(2)}, u32[]{:S(2)}) collective-permute-start(bf16[2,64,640]{2,1,0:T(8,128)(2,1)S(1)} %collective-permute-done.10.refs_0_), channel_id=1, source_target_pairs={{0,2},{2,0},{4,6},{6,4},{8,10},{10,8},{12,14},{14,12},{1,3},{3,1},... | collective-permute-start | bytes 491528 | tf_op jit(solution)/shard_map/ppermute | solution.py:287
  56.4 1.4 %collective-permute-start.14 = (bf16[2,64,640]{2,1,0:T(8,128)(2,1)S(1)}, bf16[2,64,640]{2,1,0:T(8,128)(2,1)S(1)}, u32[]{:S(2)}, u32[]{:S(2)}) collective-permute-start(bf16[2,64,640]{2,1,0:T(8,128)(2,1)S(1)} %collective-permute-done.11.refs_1_), channel_id=1, source_target_pairs={{0,2},{2,0},{4,6},{6,4},{8,10},{10,8},{12,14},{14,12},{1,3},{3,1},... | collective-permute-start | bytes 491528 | tf_op jit(solution)/shard_map/ppermute | solution.py:287
  56.4 1.6 %collective-permute-start.15 = (bf16[2,64,640]{2,1,0:T(8,128)(2,1)S(1)}, bf16[2,64,640]{2,1,0:T(8,128)(2,1)S(1)}, u32[]{:S(2)}, u32[]{:S(2)}) collective-permute-start(bf16[2,64,640]{2,1,0:T(8,128)(2,1)S(1)} %collective-permute-done.12.refs_2_), channel_id=1, source_target_pairs={{0,2},{2,0},{4,6},{6,4},{8,10},{10,8},{12,14},{14,12},{1,3},{3,1},... | collective-permute-start | bytes 491528 | tf_op jit(solution)/shard_map/ppermute | solution.py:287

commit v3 on v2

--- a/solution.py
+++ b/solution.py
@@ -87,9 +87,9 @@
 
 
 def stage_kernel(*refs):
-    slabs = (len(refs) - 6) // 2
+    slabs = (len(refs) - 4) // 2
     own, other = refs[:slabs], refs[slabs : 2 * slabs]
-    cos_ref, sin_ref, k_ref, v_ref, ck_ref, cv_ref = refs[2 * slabs :]
+    cos_ref, sin_ref, k_ref, v_ref = refs[2 * slabs :]
     me = lax.axis_index("blk")
     chip, core = me // CORES, me % CORES
     rows = own[0].shape[0]
@@ -97,15 +97,16 @@
         for piece, side in ((own[j], core), (other[j], 1 - core)):
             at = pl.multiple_of(((chip ^ j) * CORES + side) * rows, rows)
             here = pl.ds(at, rows)
-            k_ref[here] = rotate(lanes(piece, 0), cos_ref[here], sin_ref[here])
-            v_ref[here] = lanes(piece, 1)
-            ck_ref[here] = lanes(piece, 2)
-            cv_ref[here] = lanes(piece, 3)
+            new = pl.ds(pl.multiple_of(cos_ref.shape[0] + at, rows), rows)
+            k_ref[new] = rotate(lanes(piece, 0), cos_ref[here], sin_ref[here])
+            v_ref[new] = lanes(piece, 1)
+            k_ref[here] = lanes(piece, 2)
+            v_ref[here] = lanes(piece, 3)
 
 
 def attend_kernel(group, own_half, *refs):
-    queries, rest = refs[:-9], refs[-9:]
-    k_ref, v_ref, ck_ref, cv_ref, cos_ref, sin_ref, ctx_ref, out_ref, q_s = rest
+    queries, rest = refs[:-7], refs[-7:]
+    k_ref, v_ref, cos_ref, sin_ref, ctx_ref, out_ref, q_s = rest
     slabs = len(queries)
     me = lax.axis_index("blk")
     chip, core = me // CORES, me % CORES
@@ -126,8 +127,9 @@
     scale = math.log2(math.e) / math.sqrt(HEAD_SIZE)
     height = group * rows
     total_rows = slabs * span
-    cached_ok = lax.broadcasted_iota(jnp.int32, (1, total_rows), 1) < ctx_ref[0]
-    cached_bias = jnp.where(cached_ok, 0.0, NEG_FILL).astype(jnp.float32)
+    place = lax.broadcasted_iota(jnp.int32, (1, 2 * total_rows), 1)
+    hidden = jnp.logical_and(place >= ctx_ref[0], place < total_rows)
+    bias = jnp.where(hidden, NEG_FILL, 0.0).astype(jnp.float32)
     row = lax.broadcasted_iota(jnp.int32, (height, span), 0) % rows + core * rows
     col = lax.broadcasted_iota(jnp.int32, (height, span), 1)
     diagonal = col <= row
@@ -139,13 +141,11 @@
     def attend(blocks):
         for n, block in enumerate(blocks):
             q = q_s[block * height : (block + 1) * height]
-            begin, end = block * span, (block + 1) * span
+            begin, end = total_rows + block * span, total_rows + (block + 1) * span
             parts = [
-                (scores_of(q, ck_ref[...]) + cached_bias, cv_ref[...]),
+                (scores_of(q, k_ref[:begin]) + bias[:, :begin], v_ref[:begin]),
                 (jnp.where(diagonal, scores_of(q, k_ref[begin:end]), NEG_FILL), v_ref[begin:end]),
             ]
-            if block:
-                parts.append((scores_of(q, k_ref[:begin]), v_ref[:begin]))
             top = functools.reduce(jnp.maximum, [jnp.max(scores, axis=1, keepdims=True) for scores, _ in parts])
             total, summed = 0.0, 0.0
             for scores, values in parts:
@@ -241,12 +241,12 @@
     swapped = [lax.ppermute(x, "blk", partner) for x in keys]
     half_chips = chips // 2
 
-    lined = jax.ShapeDtypeStruct((total_rows, HEAD_SIZE), jnp.bfloat16)
+    lined = jax.ShapeDtypeStruct((2 * total_rows, HEAD_SIZE), jnp.bfloat16)
     staged = pl.pallas_call(
         stage_kernel,
-        out_shape=[lined] * 4,
+        out_shape=[lined] * 2,
         in_specs=[whole()] * (2 * chips + 2),
-        out_specs=[whole()] * 4,
+        out_specs=[whole()] * 2,
         name="stage",
         compiler_params=room(8),
         cost_estimate=pl.CostEstimate(flops=1_000_000, bytes_accessed=1_000_000, transcendentals=0),
@@ -256,7 +256,7 @@
         return pl.pallas_call(
             functools.partial(attend_kernel, group, own_half),
             out_shape=jax.ShapeDtypeStruct((half_chips, rows, width), jnp.bfloat16),
-            in_specs=[whole()] * (chips + 6) + [whole(pltpu.SMEM)],
+            in_specs=[whole()] * (chips + 4) + [whole(pltpu.SMEM)],
             out_specs=whole(),
             scratch_shapes=[pltpu.VMEM((chips * group * rows, HEAD_SIZE), jnp.bfloat16)],
             name="attend",

time: 60.4 us -> 60.4 us (level)
  no operation moved by 1% of the time
where the time goes in v3:
time: 60.4 us; the launch traced here: 59.9 us
  starting transfers between devices  23.8 us (39%)
  waiting for transfers between devices  23.3 us (39%)
  Pallas kernels  9.98 us (17%)
  between operations  1.55 us (3%)
  other arithmetic  1.25 us (2%)
    ppermute x3, waiting for transfers between devices, head_sharded(): pieces = [kept] + [lax.ppermute(kept, 'blk', along(j)) for j in (1, 2, 3)]  7.73 us
    ppermute x1, waiting for transfers between devices, head_sharded(): far = lax.ppermute(sent, 'blk', along(2))  6.28 us
    ppermute x3, starting transfers between devices, head_sharded(): lax.ppermute(keyed[j], 'blk', along(j))  5.71 us
    ppermute x3, waiting for transfers between devices, head_sharded(): lax.ppermute(asked[j], 'blk', along(j))  4.97 us
    ppermute x3, starting transfers between devices, head_sharded(): lax.ppermute(asked[j], 'blk', along(j))  4.45 us
    ppermute x3, starting transfers between devices, head_sharded(): pieces = [kept] + [lax.ppermute(kept, 'blk', along(j)) for j in (1, 2, 3)]  4.45 us
    pallas_call x6, Pallas kernels, project(): pl.pallas_call(functools.partial(project_kernel, distances, final, column...  4.26 us
    pallas_call x2, Pallas kernels, attend(): pl.pallas_call(functools.partial(attend_kernel, group, own_half), out_sha...  2.95 us
  transfers between devices with their start and end apart: 28, of which 10 were waited for; matrix products, arithmetic and copies ran while one was open for 2% of the time, Pallas kernels for 9%

profile of v3, /device:TPU:0, one launch (start us, length us, event | category | flops | bytes accessed | tf_op | source)
XLA Modules:
  0.0 59.9 jit_solution(16352887068562199425)
XLA Ops:
  0.0 1.3 %shard_map.83 = (bf16[64,512]{1,0:T(8,128)(2,1)S(1)}, bf16[64,512]{1,0:T(8,128)(2,1)S(1)}, bf16[64,512]{1,0:T(8,128)(2,1)S(1)}, bf16[64,512]{1,0:T(8,128)(2,1)S(1)}) custom-call(bf16[64,512]{1,0:T(8,128)(2,1)} %refs_0_.3, bf16[64,512]{1,0:T(8,128)(2,1)} %refs_1_.1, bf16[64,512]{1,0:T(8,128)(2,1)} %refs_2_.1, bf16[64,512]{1,0:T(8,128)(2,1)} %refs_3_.1), custom_call_target="tpu_custom_call" | custom-call | tf_op jit(solution)/shard_map/pallas_call | solution.py:66
  1.3 3.1 %collective-permute-start.3 = (bf16[64,512]{1,0:T(8,128)(2,1)S(1)}, bf16[64,512]{1,0:T(8,128)(2,1)S(1)}, u32[]{:S(2)}, u32[]{:S(2)}) collective-permute-start(bf16[64,512]{1,0:T(8,128)(2,1)S(1)} %get-tuple-element.26), channel_id=1, source_target_pairs={{0,4},{2,6},{4,0},{6,2},{8,12},{10,14},{12,8},{14,10},{1,5},{3,7},... | collective-permute-start | bytes 196616 | tf_op jit(solution)/shard_map/ppermute | solution.py:237
  4.4 2.6 %collective-permute-start.4 = (bf16[64,512]{1,0:T(8,128)(2,1)S(1)}, bf16[64,512]{1,0:T(8,128)(2,1)S(1)}, u32[]{:S(2)}, u32[]{:S(2)}) collective-permute-start(bf16[64,512]{1,0:T(8,128)(2,1)S(1)} %get-tuple-element.31), channel_id=1, source_target_pairs={{0,8},{2,10},{4,12},{6,14},{8,0},{10,2},{12,4},{14,6},{1,9},{3,11}... | collective-permute-start | bytes 196616 | tf_op jit(solution)/shard_map/ppermute | solution.py:237
  7.0 0.0 collective-permute-start.5
  7.7 0.0 copy-start
  7.7 1.0 %fusion = (f32[512,64]{1,0:T(8,128)S(1)}, f32[512,64]{1,0:T(8,128)S(1)}, f32[512,64]{1,0:T(8,128)S(1)}) fusion(f32[64]{0:T(128)S(1)} %negate_power_fusion, f32[512]{0:T(512)S(1)} %add_convert_fusion), kind=kLoop, calls=%fused_computation.5 | loop fusion | flops 65536 | bytes 395520 | tf_op jit(solution)/shard_map/neg | solution.py:235
  8.7 0.2 pad_maximum_fusion.1
  8.9 0.0 collective-permute-done.3.refs_1_
  8.9 0.1 collective-permute-start.6
  9.0 0.5 collective-permute-start.7
  9.5 1.3 %shard_map.82 = (bf16[64,640]{1,0:T(8,128)(2,1)S(1)}, bf16[64,640]{1,0:T(8,128)(2,1)S(1)}, bf16[64,640]{1,0:T(8,128)(2,1)S(1)}, bf16[64,640]{1,0:T(8,128)(2,1)S(1)}) custom-call(bf16[64,2560]{1,0:T(8,128)(2,1)} %refs_0_.2), custom_call_target="tpu_custom_call" | custom-call | tf_op jit(solution)/shard_map/pallas_call | solution.py:66
  10.9 1.0 %collective-permute-start = (bf16[64,640]{1,0:T(8,128)(2,1)S(1)}, bf16[64,640]{1,0:T(8,128)(2,1)S(1)}, u32[]{:S(2)}, u32[]{:S(2)}) collective-permute-start(bf16[64,640]{1,0:T(8,128)(2,1)S(1)} %get-tuple-element.22), channel_id=1, source_target_pairs={{0,4},{2,6},{4,0},{6,2},{8,12},{10,14},{12,8},{14,10},{1,5},{3,7},... | collective-permute-start | bytes 245768 | tf_op jit(solution)/shard_map/ppermute | solution.py:238
  11.8 3.5 %collective-permute-start.1 = (bf16[64,640]{1,0:T(8,128)(2,1)S(1)}, bf16[64,640]{1,0:T(8,128)(2,1)S(1)}, u32[]{:S(2)}, u32[]{:S(2)}) collective-permute-start(bf16[64,640]{1,0:T(8,128)(2,1)S(1)} %get-tuple-element.23), channel_id=1, source_target_pairs={{0,8},{2,10},{4,12},{6,14},{8,0},{10,2},{12,4},{14,6},{1,9},{3,11}... | collective-permute-start | bytes 245768 | tf_op jit(solution)/shard_map/ppermute | solution.py:238
  15.3 0.0 collective-permute-start.2
  15.3 0.1 collective-permute-start.8
  15.4 0.5 collective-permute-start.9
  16.6 0.1 collective-permute-done.8.refs_6_
  16.6 0.2 collective-permute-done.9.refs_7_
  16.8 0.1 stage.1
  16.9 5.0 %collective-permute-done.1.refs_2_ = bf16[64,640]{1,0:T(8,128)(2,1)S(1)} collective-permute-done((bf16[64,640]{1,0:T(8,128)(2,1)S(1)}, bf16[64,640]{1,0:T(8,128)(2,1)S(1)}, u32[]{:S(2)}, u32[]{:S(2)}) %collective-permute-start.1) | collective-permute-done | bytes 81952 | tf_op jit(solution)/shard_map/ppermute | solution.py:238
  21.9 1.6 %attend.3.refs_0_ = bf16[2,64,640]{2,1,0:T(8,128)(2,1)S(1)} custom-call(bf16[64,640]{1,0:T(8,128)(2,1)S(1)} %get-tuple-element.21.refs_0_, bf16[64,640]{1,0:T(8,128)(2,1)S(1)} %collective-permute-done.refs_1_, bf16[64,640]{1,0:T(8,128)(2,1)S(1)} %collective-permute-done.1.refs_2_, bf16[64,640]{1,0:T(8,128)(2,1)S(1)} %collective-permute-done.2.refs_3_, ...), custom_call_target="tpu_custom_call" | custom-call | flops 400000000 | bytes 1000000 | tf_op jit(solution)/shard_map/attend/pallas_call | solution.py:256
  23.5 2.7 %collective-permute-start.17 = (bf16[2,64,640]{2,1,0:T(8,128)(2,1)S(1)}, bf16[2,64,640]{2,1,0:T(8,128)(2,1)S(1)}, u32[]{:S(2)}, u32[]{:S(2)}) collective-permute-start(bf16[2,64,640]{2,1,0:T(8,128)(2,1)S(1)} %attend.3.refs_0_), channel_id=1, source_target_pairs={{0,8},{2,10},{4,12},{6,14},{8,0},{10,2},{12,4},{14,6},{1,9},{3,11}... | collective-permute-start | bytes 491528 | tf_op jit(solution)/shard_map/ppermute | solution.py:290
  26.2 0.6 collective-permute-start.20
  26.8 6.3 %collective-permute-done.17.refs_1_ = bf16[2,64,640]{2,1,0:T(8,128)(2,1)S(1)} collective-permute-done((bf16[2,64,640]{2,1,0:T(8,128)(2,1)S(1)}, bf16[2,64,640]{2,1,0:T(8,128)(2,1)S(1)}, u32[]{:S(2)}, u32[]{:S(2)}) %collective-permute-start.17) | collective-permute-done | bytes 163872 | tf_op jit(solution)/shard_map/ppermute | solution.py:290
  33.1 0.2 collective-permute-start.18
  33.3 1.8 %collective-permute-done.20.refs_0_ = bf16[2,64,640]{2,1,0:T(8,128)(2,1)S(1)} collective-permute-done((bf16[2,64,640]{2,1,0:T(8,128)(2,1)S(1)}, bf16[2,64,640]{2,1,0:T(8,128)(2,1)S(1)}, u32[]{:S(2)}, u32[]{:S(2)}) %collective-permute-start.20) | collective-permute-done | bytes 163872 | tf_op jit(solution)/shard_map/ppermute | solution.py:291
  35.1 0.5 collective-permute-start.22
  35.6 0.8 %collective-permute-start.25 = (bf16[1,64,640]{2,1,0:T(8,128)(2,1)S(1)}, bf16[1,64,640]{2,1,0:T(8,128)(2,1)S(1)}, u32[]{:S(2)}, u32[]{:S(2)}) collective-permute-start(bf16[1,64,640]{2,1,0:T(8,128)(2,1)S(1)} %get-tuple-element.38), channel_id=1, source_target_pairs={{0,4},{2,6},{4,0},{6,2},{8,12},{10,14},{12,8},{14,10},{1,5},{3,7},... | collective-permute-start | bytes 245768 | tf_op jit(solution)/shard_map/ppermute | solution.py:298
  36.4 1.4 %attend.2.refs_0_ = bf16[2,64,640]{2,1,0:T(8,128)(2,1)S(1)} custom-call(bf16[64,640]{1,0:T(8,128)(2,1)S(1)} %get-tuple-element.21.refs_0_, bf16[64,640]{1,0:T(8,128)(2,1)S(1)} %collective-permute-done.refs_1_, bf16[64,640]{1,0:T(8,128)(2,1)S(1)} %collective-permute-done.1.refs_2_, bf16[64,640]{1,0:T(8,128)(2,1)S(1)} %collective-permute-done.2.refs_3_, ...), custom_call_target="tpu_custom_call" | custom-call | flops 400000000 | bytes 1000000 | tf_op jit(solution)/shard_map/attend/pallas_call | solution.py:256
  37.8 0.1 collective-permute-start.16
  37.9 0.5 collective-permute-start.19
  38.4 1.6 %collective-permute-done.25.refs_0_ = bf16[1,64,640]{2,1,0:T(8,128)(2,1)S(1)} collective-permute-done((bf16[1,64,640]{2,1,0:T(8,128)(2,1)S(1)}, bf16[1,64,640]{2,1,0:T(8,128)(2,1)S(1)}, u32[]{:S(2)}, u32[]{:S(2)}) %collective-permute-start.25) | collective-permute-done | bytes 81952 | tf_op jit(solution)/shard_map/ppermute | solution.py:298
  40.0 0.5 project.7.refs_4_
  40.5 0.9 %collective-permute-start.10 = (bf16[2,64,640]{2,1,0:T(8,128)(2,1)S(1)}, bf16[2,64,640]{2,1,0:T(8,128)(2,1)S(1)}, u32[]{:S(2)}, u32[]{:S(2)}) collective-permute-start(bf16[2,64,640]{2,1,0:T(8,128)(2,1)S(1)} %attend.2.refs_0_), channel_id=1, source_target_pairs={{0,4},{2,6},{4,0},{6,2},{8,12},{10,14},{12,8},{14,10},{1,5},{3,7},... | collective-permute-start | bytes 491528 | tf_op jit(solution)/shard_map/ppermute | solution.py:303
  41.4 1.1 %collective-permute-start.11 = (bf16[2,64,640]{2,1,0:T(8,128)(2,1)S(1)}, bf16[2,64,640]{2,1,0:T(8,128)(2,1)S(1)}, u32[]{:S(2)}, u32[]{:S(2)}) collective-permute-start(bf16[2,64,640]{2,1,0:T(8,128)(2,1)S(1)} %attend.2.refs_0_), channel_id=1, source_target_pairs={{0,8},{2,10},{4,12},{6,14},{8,0},{10,2},{12,4},{14,6},{1,9},{3,11}... | collective-permute-start | bytes 491528 | tf_op jit(solution)/shard_map/ppermute | solution.py:303
  42.5 2.5 %collective-permute-start.12 = (bf16[2,64,640]{2,1,0:T(8,128)(2,1)S(1)}, bf16[2,64,640]{2,1,0:T(8,128)(2,1)S(1)}, u32[]{:S(2)}, u32[]{:S(2)}) collective-permute-start(bf16[2,64,640]{2,1,0:T(8,128)(2,1)S(1)} %attend.2.refs_0_), channel_id=1, source_target_pairs={{0,12},{2,14},{4,8},{6,10},{8,4},{10,6},{12,0},{14,2},{1,13},{3,15... | collective-permute-start | bytes 491528 | tf_op jit(solution)/shard_map/ppermute | solution.py:303
  45.0 0.8 %project.8.refs_2_ = f32[640,256]{1,0:T(8,128)S(1)} custom-call(bf16[640,2560]{1,0:T(8,128)(2,1)S(1)} %copy-done, bf16[2,64,640]{2,1,0:T(8,128)(2,1)S(1)} %collective-permute-done.20.refs_0_, bf16[2,64,640]{2,1,0:T(8,128)(2,1)S(1)} %collective-permute-done.17.refs_1_, bf16[2,64,640]{2,1,0:T(8,128)(2,1)S(1)} %collective-permute-done.21.refs_2_, ...), custom_call_target="tpu_custom_call" | custom-call | flops 419430400 | bytes 1000000 | tf_op jit(solution)/shard_map/project/pallas_call | solution.py:273
  45.8 0.4 project.9
  46.2 1.3 %collective-permute-start.24 = (bf16[640,128]{1,0:T(8,128)(2,1)S(1)}, bf16[640,128]{1,0:T(8,128)(2,1)S(1)}, u32[]{:S(2)}, u32[]{:S(2)}) collective-permute-start(bf16[640,128]{1,0:T(8,128)(2,1)S(1)} %project.9), channel_id=1, source_target_pairs={{0,1},{1,0},{2,3},{3,2},{4,5},{5,4},{6,7},{7,6},{8,9},{9,8},{10,11... | collective-permute-start | bytes 491528 | tf_op jit(solution)/shard_map/ppermute | solution.py:301
  47.4 0.4 project.10
  47.9 0.9 %collective-permute-start.27 = (bf16[640,128]{1,0:T(8,128)(2,1)S(1)}, bf16[640,128]{1,0:T(8,128)(2,1)S(1)}, u32[]{:S(2)}, u32[]{:S(2)}) collective-permute-start(bf16[640,128]{1,0:T(8,128)(2,1)S(1)} %project.10), channel_id=1, source_target_pairs={{0,1},{1,0},{2,3},{3,2},{4,5},{5,4},{6,7},{7,6},{8,9},{9,8},{10,11... | collective-permute-start | bytes 491528 | tf_op jit(solution)/shard_map/ppermute | solution.py:301
  48.7 1.0 %collective-permute-done.10.refs_0_ = bf16[2,64,640]{2,1,0:T(8,128)(2,1)S(1)} collective-permute-done((bf16[2,64,640]{2,1,0:T(8,128)(2,1)S(1)}, bf16[2,64,640]{2,1,0:T(8,128)(2,1)S(1)}, u32[]{:S(2)}, u32[]{:S(2)}) %collective-permute-start.10) | collective-permute-done | bytes 163872 | tf_op jit(solution)/shard_map/ppermute | solution.py:303
  49.8 6.7 %collective-permute-done.11.refs_1_ = bf16[2,64,640]{2,1,0:T(8,128)(2,1)S(1)} collective-permute-done((bf16[2,64,640]{2,1,0:T(8,128)(2,1)S(1)}, bf16[2,64,640]{2,1,0:T(8,128)(2,1)S(1)}, u32[]{:S(2)}, u32[]{:S(2)}) %collective-permute-start.11) | collective-permute-done | bytes 163872 | tf_op jit(solution)/shard_map/ppermute | solution.py:303
  56.5 0.5 collective-permute-start.15
  57.0 0.5 project.6.refs_6_
  57.6 0.3 collective-permute-done.14.refs_4_
  57.9 0.2 collective-permute-done.15.refs_5_
  58.1 1.7 %project.11 = bf16[640,256]{1,0:T(8,128)(2,1)} custom-call(bf16[640,2560]{1,0:T(8,128)(2,1)S(1)} %copy-done, bf16[2,64,640]{2,1,0:T(8,128)(2,1)S(1)} %collective-permute-done.10.refs_0_, bf16[2,64,640]{2,1,0:T(8,128)(2,1)S(1)} %collective-permute-done.11.refs_1_, bf16[2,64,640]{2,1,0:T(8,128)(2,1)S(1)} %collective-permute-done.12.refs_2_, ...), custom_call_target="tpu_custom_call" | custom-call | flops 629145600 | bytes 1000000 | tf_op jit(solution)/shard_map/project/pallas_call | solution.py:273
  (27 shorter events, 0.1 us)
Async XLA Ops:
  1.3 7.6 %collective-permute-start.3 = (bf16[64,512]{1,0:T(8,128)(2,1)S(1)}, bf16[64,512]{1,0:T(8,128)(2,1)S(1)}, u32[]{:S(2)}, u32[]{:S(2)}) collective-permute-start(bf16[64,512]{1,0:T(8,128)(2,1)S(1)} %get-tuple-element.26), channel_id=1, source_target_pairs={{0,4},{2,6},{4,0},{6,2},{8,12},{10,14},{12,8},{14,10},{1,5},{3,7},... | collective-permute-start | bytes 196616 | tf_op jit(solution)/shard_map/ppermute | solution.py:237
  4.4 7.4 %collective-permute-start.4 = (bf16[64,512]{1,0:T(8,128)(2,1)S(1)}, bf16[64,512]{1,0:T(8,128)(2,1)S(1)}, u32[]{:S(2)}, u32[]{:S(2)}) collective-permute-start(bf16[64,512]{1,0:T(8,128)(2,1)S(1)} %get-tuple-element.31), channel_id=1, source_target_pairs={{0,8},{2,10},{4,12},{6,14},{8,0},{10,2},{12,4},{14,6},{1,9},{3,11}... | collective-permute-start | bytes 196616 | tf_op jit(solution)/shard_map/ppermute | solution.py:237
  7.0 8.3 %collective-permute-start.5 = (bf16[64,512]{1,0:T(8,128)(2,1)S(1)}, bf16[64,512]{1,0:T(8,128)(2,1)S(1)}, u32[]{:S(2)}, u32[]{:S(2)}) collective-permute-start(bf16[64,512]{1,0:T(8,128)(2,1)S(1)} %get-tuple-element.32), channel_id=1, source_target_pairs={{0,12},{2,14},{4,8},{6,10},{8,4},{10,6},{12,0},{14,2},{1,13},{3,15... | collective-permute-start | bytes 196616 | tf_op jit(solution)/shard_map/ppermute | solution.py:237
  7.7 32.3 %copy-start = (bf16[640,2560]{1,0:T(8,128)(2,1)S(1)}, bf16[640,2560]{1,0:T(8,128)(2,1)}, u32[]{:S(2)}) copy-start(bf16[640,2560]{1,0:T(8,128)(2,1)} %w_ref.11) | copy-start | bytes 9830404
  8.9 6.4 %collective-permute-start.6 = (bf16[64,512]{1,0:T(8,128)(2,1)S(1)}, bf16[64,512]{1,0:T(8,128)(2,1)S(1)}, u32[]{:S(2)}, u32[]{:S(2)}) collective-permute-start(bf16[64,512]{1,0:T(8,128)(2,1)S(1)} %get-tuple-element.29.refs_0_), channel_id=1, source_target_pairs={{0,2},{2,0},{4,6},{6,4},{8,10},{10,8},{12,14},{14,12},{1,3},{3,1},... | collective-permute-start | bytes 196616 | tf_op jit(solution)/shard_map/ppermute | solution.py:241
  9.0 6.4 %collective-permute-start.7 = (bf16[64,512]{1,0:T(8,128)(2,1)S(1)}, bf16[64,512]{1,0:T(8,128)(2,1)S(1)}, u32[]{:S(2)}, u32[]{:S(2)}) collective-permute-start(bf16[64,512]{1,0:T(8,128)(2,1)S(1)} %collective-permute-done.3.refs_1_), channel_id=1, source_target_pairs={{0,2},{2,0},{4,6},{6,4},{8,10},{10,8},{12,14},{14,12},{1,3},{3,1},... | collective-permute-start | bytes 196616 | tf_op jit(solution)/shard_map/ppermute | solution.py:241
  10.9 6.1 %collective-permute-start = (bf16[64,640]{1,0:T(8,128)(2,1)S(1)}, bf16[64,640]{1,0:T(8,128)(2,1)S(1)}, u32[]{:S(2)}, u32[]{:S(2)}) collective-permute-start(bf16[64,640]{1,0:T(8,128)(2,1)S(1)} %get-tuple-element.22), channel_id=1, source_target_pairs={{0,4},{2,6},{4,0},{6,2},{8,12},{10,14},{12,8},{14,10},{1,5},{3,7},... | collective-permute-start | bytes 245768 | tf_op jit(solution)/shard_map/ppermute | solution.py:238
  11.8 10.1 %collective-permute-start.1 = (bf16[64,640]{1,0:T(8,128)(2,1)S(1)}, bf16[64,640]{1,0:T(8,128)(2,1)S(1)}, u32[]{:S(2)}, u32[]{:S(2)}) collective-permute-start(bf16[64,640]{1,0:T(8,128)(2,1)S(1)} %get-tuple-element.23), channel_id=1, source_target_pairs={{0,8},{2,10},{4,12},{6,14},{8,0},{10,2},{12,4},{14,6},{1,9},{3,11}... | collective-permute-start | bytes 245768 | tf_op jit(solution)/shard_map/ppermute | solution.py:238
  15.3 6.6 %collective-permute-start.2 = (bf16[64,640]{1,0:T(8,128)(2,1)S(1)}, bf16[64,640]{1,0:T(8,128)(2,1)S(1)}, u32[]{:S(2)}, u32[]{:S(2)}) collective-permute-start(bf16[64,640]{1,0:T(8,128)(2,1)S(1)} %get-tuple-element.24), channel_id=1, source_target_pairs={{0,12},{2,14},{4,8},{6,10},{8,4},{10,6},{12,0},{14,2},{1,13},{3,15... | collective-permute-start | bytes 245768 | tf_op jit(solution)/shard_map/ppermute | solution.py:238
  15.3 1.3 %collective-permute-start.8 = (bf16[64,512]{1,0:T(8,128)(2,1)S(1)}, bf16[64,512]{1,0:T(8,128)(2,1)S(1)}, u32[]{:S(2)}, u32[]{:S(2)}) collective-permute-start(bf16[64,512]{1,0:T(8,128)(2,1)S(1)} %collective-permute-done.4.refs_2_), channel_id=1, source_target_pairs={{0,2},{2,0},{4,6},{6,4},{8,10},{10,8},{12,14},{14,12},{1,3},{3,1},... | collective-permute-start | bytes 196616 | tf_op jit(solution)/shard_map/ppermute | solution.py:241
  15.4 1.4 %collective-permute-start.9 = (bf16[64,512]{1,0:T(8,128)(2,1)S(1)}, bf16[64,512]{1,0:T(8,128)(2,1)S(1)}, u32[]{:S(2)}, u32[]{:S(2)}) collective-permute-start(bf16[64,512]{1,0:T(8,128)(2,1)S(1)} %collective-permute-done.5.refs_3_), channel_id=1, source_target_pairs={{0,2},{2,0},{4,6},{6,4},{8,10},{10,8},{12,14},{14,12},{1,3},{3,1},... | collective-permute-start | bytes 196616 | tf_op jit(solution)/shard_map/ppermute | solution.py:241
  23.5 9.6 %collective-permute-start.17 = (bf16[2,64,640]{2,1,0:T(8,128)(2,1)S(1)}, bf16[2,64,640]{2,1,0:T(8,128)(2,1)S(1)}, u32[]{:S(2)}, u32[]{:S(2)}) collective-permute-start(bf16[2,64,640]{2,1,0:T(8,128)(2,1)S(1)} %attend.3.refs_0_), channel_id=1, source_target_pairs={{0,8},{2,10},{4,12},{6,14},{8,0},{10,2},{12,4},{14,6},{1,9},{3,11}... | collective-permute-start | bytes 491528 | tf_op jit(solution)/shard_map/ppermute | solution.py:290
  26.2 11.6 %collective-permute-start.23 = (bf16[2,64,640]{2,1,0:T(8,128)(2,1)S(1)}, bf16[2,64,640]{2,1,0:T(8,128)(2,1)S(1)}, u32[]{:S(2)}, u32[]{:S(2)}) collective-permute-start(bf16[2,64,640]{2,1,0:T(8,128)(2,1)S(1)} %attend.3.refs_0_), channel_id=1, source_target_pairs={{0,2},{2,0},{4,6},{6,4},{8,10},{10,8},{12,14},{14,12},{1,3},{3,1},... | collective-permute-start | bytes 491528 | tf_op jit(solution)/shard_map/ppermute | solution.py:287
  26.2 8.9 %collective-permute-start.20 = (bf16[2,64,640]{2,1,0:T(8,128)(2,1)S(1)}, bf16[2,64,640]{2,1,0:T(8,128)(2,1)S(1)}, u32[]{:S(2)}, u32[]{:S(2)}) collective-permute-start(bf16[2,64,640]{2,1,0:T(8,128)(2,1)S(1)} %attend.3.refs_0_), channel_id=1, source_target_pairs={{0,4},{2,6},{4,0},{6,2},{8,12},{10,14},{12,8},{14,10},{1,5},{3,7},... | collective-permute-start | bytes 491528 | tf_op jit(solution)/shard_map/ppermute | solution.py:291
  33.1 4.8 %collective-permute-start.18 = (bf16[1,64,640]{2,1,0:T(8,128)(2,1)S(1)}, bf16[1,64,640]{2,1,0:T(8,128)(2,1)S(1)}, u32[]{:S(2)}, u32[]{:S(2)}) collective-permute-start(bf16[1,64,640]{2,1,0:T(8,128)(2,1)S(1)} %get-tuple-element.37), channel_id=1, source_target_pairs={{0,4},{2,6},{4,0},{6,2},{8,12},{10,14},{12,8},{14,10},{1,5},{3,7},... | collective-permute-start | bytes 245768 | tf_op jit(solution)/shard_map/ppermute | solution.py:298
  35.1 6.4 %collective-permute-start.21 = (bf16[2,64,640]{2,1,0:T(8,128)(2,1)S(1)}, bf16[2,64,640]{2,1,0:T(8,128)(2,1)S(1)}, u32[]{:S(2)}, u32[]{:S(2)}) collective-permute-start(bf16[2,64,640]{2,1,0:T(8,128)(2,1)S(1)} %collective-permute-done.20.refs_0_), channel_id=1, source_target_pairs={{0,2},{2,0},{4,6},{6,4},{8,10},{10,8},{12,14},{14,12},{1,3},{3,1},... | collective-permute-start | bytes 491528 | tf_op jit(solution)/shard_map/ppermute | solution.py:287
  35.1 7.4 %collective-permute-start.22 = (bf16[2,64,640]{2,1,0:T(8,128)(2,1)S(1)}, bf16[2,64,640]{2,1,0:T(8,128)(2,1)S(1)}, u32[]{:S(2)}, u32[]{:S(2)}) collective-permute-start(bf16[2,64,640]{2,1,0:T(8,128)(2,1)S(1)} %collective-permute-done.17.refs_1_), channel_id=1, source_target_pairs={{0,2},{2,0},{4,6},{6,4},{8,10},{10,8},{12,14},{14,12},{1,3},{3,1},... | collective-permute-start | bytes 491528 | tf_op jit(solution)/shard_map/ppermute | solution.py:287
  35.6 4.4 %collective-permute-start.25 = (bf16[1,64,640]{2,1,0:T(8,128)(2,1)S(1)}, bf16[1,64,640]{2,1,0:T(8,128)(2,1)S(1)}, u32[]{:S(2)}, u32[]{:S(2)}) collective-permute-start(bf16[1,64,640]{2,1,0:T(8,128)(2,1)S(1)} %get-tuple-element.38), channel_id=1, source_target_pairs={{0,4},{2,6},{4,0},{6,2},{8,12},{10,14},{12,8},{14,10},{1,5},{3,7},... | collective-permute-start | bytes 245768 | tf_op jit(solution)/shard_map/ppermute | solution.py:298
  37.8 10.0 %collective-permute-start.16 = (bf16[2,64,640]{2,1,0:T(8,128)(2,1)S(1)}, bf16[2,64,640]{2,1,0:T(8,128)(2,1)S(1)}, u32[]{:S(2)}, u32[]{:S(2)}) collective-permute-start(bf16[2,64,640]{2,1,0:T(8,128)(2,1)S(1)} %attend.2.refs_0_), channel_id=1, source_target_pairs={{0,2},{2,0},{4,6},{6,4},{8,10},{10,8},{12,14},{14,12},{1,3},{3,1},... | collective-permute-start | bytes 491528 | tf_op jit(solution)/shard_map/ppermute | solution.py:287
  37.9 2.6 %collective-permute-start.19 = (bf16[1,64,640]{2,1,0:T(8,128)(2,1)S(1)}, bf16[1,64,640]{2,1,0:T(8,128)(2,1)S(1)}, u32[]{:S(2)}, u32[]{:S(2)}) collective-permute-start(bf16[1,64,640]{2,1,0:T(8,128)(2,1)S(1)} %collective-permute-done.18.refs_0_), channel_id=1, source_target_pairs={{0,2},{2,0},{4,6},{6,4},{8,10},{10,8},{12,14},{14,12},{1,3},{3,1},... | collective-permute-start | bytes 245768 | tf_op jit(solution)/shard_map/ppermute | solution.py:299
  40.0 6.1 %collective-permute-start.26 = (bf16[1,64,640]{2,1,0:T(8,128)(2,1)S(1)}, bf16[1,64,640]{2,1,0:T(8,128)(2,1)S(1)}, u32[]{:S(2)}, u32[]{:S(2)}) collective-permute-start(bf16[1,64,640]{2,1,0:T(8,128)(2,1)S(1)} %collective-permute-done.25.refs_0_), channel_id=1, source_target_pairs={{0,2},{2,0},{4,6},{6,4},{8,10},{10,8},{12,14},{14,12},{1,3},{3,1},... | collective-permute-start | bytes 245768 | tf_op jit(solution)/shard_map/ppermute | solution.py:299
  40.5 9.2 %collective-permute-start.10 = (bf16[2,64,640]{2,1,0:T(8,128)(2,1)S(1)}, bf16[2,64,640]{2,1,0:T(8,128)(2,1)S(1)}, u32[]{:S(2)}, u32[]{:S(2)}) collective-permute-start(bf16[2,64,640]{2,1,0:T(8,128)(2,1)S(1)} %attend.2.refs_0_), channel_id=1, source_target_pairs={{0,4},{2,6},{4,0},{6,2},{8,12},{10,14},{12,8},{14,10},{1,5},{3,7},... | collective-permute-start | bytes 491528 | tf_op jit(solution)/shard_map/ppermute | solution.py:303
  41.4 15.0 %collective-permute-start.11 = (bf16[2,64,640]{2,1,0:T(8,128)(2,1)S(1)}, bf16[2,64,640]{2,1,0:T(8,128)(2,1)S(1)}, u32[]{:S(2)}, u32[]{:S(2)}) collective-permute-start(bf16[2,64,640]{2,1,0:T(8,128)(2,1)S(1)} %attend.2.refs_0_), channel_id=1, source_target_pairs={{0,8},{2,10},{4,12},{6,14},{8,0},{10,2},{12,4},{14,6},{1,9},{3,11}... | collective-permute-start | bytes 491528 | tf_op jit(solution)/shard_map/ppermute | solution.py:303
  42.5 14.0 %collective-permute-start.12 = (bf16[2,64,640]{2,1,0:T(8,128)(2,1)S(1)}, bf16[2,64,640]{2,1,0:T(8,128)(2,1)S(1)}, u32[]{:S(2)}, u32[]{:S(2)}) collective-permute-start(bf16[2,64,640]{2,1,0:T(8,128)(2,1)S(1)} %attend.2.refs_0_), channel_id=1, source_target_pairs={{0,12},{2,14},{4,8},{6,10},{8,4},{10,6},{12,0},{14,2},{1,13},{3,15... | collective-permute-start | bytes 491528 | tf_op jit(solution)/shard_map/ppermute | solution.py:303
  46.2 11.3 %collective-permute-start.24 = (bf16[640,128]{1,0:T(8,128)(2,1)S(1)}, bf16[640,128]{1,0:T(8,128)(2,1)S(1)}, u32[]{:S(2)}, u32[]{:S(2)}) collective-permute-start(bf16[640,128]{1,0:T(8,128)(2,1)S(1)} %project.9), channel_id=1, source_target_pairs={{0,1},{1,0},{2,3},{3,2},{4,5},{5,4},{6,7},{7,6},{8,9},{9,8},{10,11... | collective-permute-start | bytes 491528 | tf_op jit(solution)/shard_map/ppermute | solution.py:301
  47.9 9.6 %collective-permute-start.27 = (bf16[640,128]{1,0:T(8,128)(2,1)S(1)}, bf16[640,128]{1,0:T(8,128)(2,1)S(1)}, u32[]{:S(2)}, u32[]{:S(2)}) collective-permute-start(bf16[640,128]{1,0:T(8,128)(2,1)S(1)} %project.10), channel_id=1, source_target_pairs={{0,1},{1,0},{2,3},{3,2},{4,5},{5,4},{6,7},{7,6},{8,9},{9,8},{10,11... | collective-permute-start | bytes 491528 | tf_op jit(solution)/shard_map/ppermute | solution.py:301
  49.7 7.8 %collective-permute-start.13 = (bf16[2,64,640]{2,1,0:T(8,128)(2,1)S(1)}, bf16[2,64,640]{2,1,0:T(8,128)(2,1)S(1)}, u32[]{:S(2)}, u32[]{:S(2)}) collective-permute-start(bf16[2,64,640]{2,1,0:T(8,128)(2,1)S(1)} %collective-permute-done.10.refs_0_), channel_id=1, source_target_pairs={{0,2},{2,0},{4,6},{6,4},{8,10},{10,8},{12,14},{14,12},{1,3},{3,1},... | collective-permute-start | bytes 491528 | tf_op jit(solution)/shard_map/ppermute | solution.py:287
  56.5 1.4 %collective-permute-start.14 = (bf16[2,64,640]{2,1,0:T(8,128)(2,1)S(1)}, bf16[2,64,640]{2,1,0:T(8,128)(2,1)S(1)}, u32[]{:S(2)}, u32[]{:S(2)}) collective-permute-start(bf16[2,64,640]{2,1,0:T(8,128)(2,1)S(1)} %collective-permute-done.11.refs_1_), channel_id=1, source_target_pairs={{0,2},{2,0},{4,6},{6,4},{8,10},{10,8},{12,14},{14,12},{1,3},{3,1},... | collective-permute-start | bytes 491528 | tf_op jit(solution)/shard_map/ppermute | solution.py:287
  56.5 1.6 %collective-permute-start.15 = (bf16[2,64,640]{2,1,0:T(8,128)(2,1)S(1)}, bf16[2,64,640]{2,1,0:T(8,128)(2,1)S(1)}, u32[]{:S(2)}, u32[]{:S(2)}) collective-permute-start(bf16[2,64,640]{2,1,0:T(8,128)(2,1)S(1)} %collective-permute-done.12.refs_2_), channel_id=1, source_target_pairs={{0,2},{2,0},{4,6},{6,4},{8,10},{10,8},{12,14},{14,12},{1,3},{3,1},... | collective-permute-start | bytes 491528 | tf_op jit(solution)/shard_map/ppermute | solution.py:287
